TPU v7x, 128 devices: a whole 4x4x4 slice. The times are simulated.
128 devices in a mesh: tomo: 16 (over y, z), cls: 8 (over x, core).
Axes of the slice: x: 4, y: 4, z: 4, core: 2. Of those that a mesh axis runs over, the one named last changes fastest.
Arguments:
- particles: bfloat16 [1024, 64, 4096], P(('tomo', 'cls')), may hold values from -6 to 6
- inverse_noise: float32 [1024], P(('tomo', 'cls')), may hold values from 0.005 to 0.04
- tomogram: int32 [1024], P(('tomo', 'cls')), may hold values from 0 to 63, as said below
- candidates: int32 [1024, 4], P(('tomo', 'cls')), may hold values from 0 to 31, as said below
- rotations: int32 [1024, 8], P(('tomo', 'cls')), may hold values from 0 to 15, as said below
- wedge: int32 [64, 32, 32], P('tomo'), may hold values from 0 to 1
- references: bfloat16 [32, 16, 65536], P('cls'), may hold values from -8 to 8
Outputs:
- posterior: float32 [1024, 32], P(('tomo', 'cls'))
- class_sums: float32 [32, 16, 65536], P('cls', None, 'tomo')
- wedge_sums: float32 [32, 16, 1024], P('cls', None, 'tomo')
Inputs may be any that keep to these rules, and one draw needn't show every extreme that they name: The tomogram of a particle held by index t of tomo is one of t * 4 to t * 4 + 3. `candidates`: each particle lists 4 different classes: two held by each of two different indices of cls (class c is held by index c // 4). Of the 8 particles of one device, at most 4 list classes of any one index of cls, and in every row of tomo one index of cls is listed by exactly 4 particles of every device of that row. `rotations`: 8 different indices for each particle.
All inputs are finite; a program needn't handle non-finite values.
Results may differ from a plain program's by a relative error of at most 0.009.
Values may be sent and summed in bfloat16 or wider, within the bound.
No kernel may reach another device: no remote copies, remote signals or barrier semaphores. Data moves between devices by JAX's collectives and lax.ppermute only.
A program may use at most 256 MiB of HBM per device.

v0:
```python
import math

import jax
import jax.numpy as jnp
from jax import lax
from jax.sharding import PartitionSpec as P

KB = 32
NSET = 16
ROT = 8
CAND = 4


HIGHEST = lax.Precision.HIGHEST


def dft_tables(length, band_size):
    frequency = jnp.arange(band_size, dtype=jnp.int32) - band_size // 2
    position = jnp.arange(length, dtype=jnp.int32)
    residue = jnp.mod(frequency, length)[:, None] * position[None, :] % length
    radians = residue.astype(jnp.float32) * (2.0 * math.pi / length)
    factor = 1.0 / math.sqrt(length)
    return (jnp.cos(radians) * factor, -jnp.sin(radians) * factor)


def band_spectra(volumes):
    volume_count, length, plane_size = volumes.shape
    cosine, sine = dft_tables(length, KB)
    values = volumes.astype(jnp.float32)
    first_re = jnp.einsum("jn,pnq->pjq", cosine, values, precision=HIGHEST)
    first_im = jnp.einsum("jn,pnq->pjq", sine, values, precision=HIGHEST)
    stacked = jnp.stack([first_re, first_im]).reshape(2, volume_count, KB, length, length)
    cos_part = jnp.einsum("kn,apjnz->apjkz", cosine, stacked, precision=HIGHEST)
    sin_part = jnp.einsum("kn,apjnz->apjkz", sine, stacked, precision=HIGHEST)
    second = jnp.stack([cos_part[0] - sin_part[1], cos_part[1] + sin_part[0]])
    cos_last = jnp.einsum("apjkn,ln->apjkl", second, cosine, precision=HIGHEST)
    sin_last = jnp.einsum("apjkn,ln->apjkl", second, sine, precision=HIGHEST)
    real_part = cos_last[0] - sin_last[1]
    imag_part = cos_last[1] + sin_last[0]
    return jnp.stack([real_part, imag_part], axis=1)


def indicator(labels, width):
    return (labels[:, None] == jnp.arange(width, dtype=jnp.int32)[None, :]).astype(jnp.float32)


def score_slots(inner, slot_details, quadratic, class_base, class_count, tomo_count):
    slot_count = inner.shape[0]
    slot_codes = slot_details.astype(jnp.int32)
    cand_codes = slot_codes[:, :CAND]
    rot_codes = slot_codes[:, CAND : CAND + ROT]
    tomo_hot = indicator(slot_codes[:, CAND + ROT], tomo_count)
    penalty = jnp.dot(tomo_hot, quadratic.T, precision=HIGHEST)
    table = (inner - 0.5 * penalty).reshape(slot_count, class_count, NSET)
    class_hot = (
        cand_codes[:, :, None]
        == class_base + jnp.arange(class_count, dtype=jnp.int32)[None, None, :]
    ).astype(jnp.float32)
    rot_hot = (rot_codes[:, :, None] == jnp.arange(NSET, dtype=jnp.int32)[None, None, :]).astype(
        jnp.float32
    )
    raw_slots = jnp.einsum("sjc,srn,scn->sjr", class_hot, rot_hot, table, precision=HIGHEST)
    return (raw_slots, class_hot, rot_hot, tomo_hot)


def posterior_weights(raw_own, inverse_noise):
    part_count = raw_own.shape[0]
    logits = inverse_noise[:, None] * raw_own.reshape(part_count, CAND * ROT)
    return jax.nn.softmax(logits, axis=-1)


def body(particles, inverse_noise, tomogram, candidates, rotations, wedge, references):
    part_count = particles.shape[0]
    class_count = references.shape[0]
    tomo_count = wedge.shape[0]
    class_base = lax.axis_index("cls") * class_count
    wedge_rows = wedge.reshape(tomo_count, KB * KB).astype(jnp.float32)
    local_tomo = tomogram - lax.axis_index("tomo") * tomo_count
    own_masks = jnp.dot(indicator(local_tomo, tomo_count), wedge_rows, precision=HIGHEST)
    spectra = band_spectra(particles).astype(jnp.bfloat16)
    masked = (spectra * own_masks.reshape(part_count, 1, KB, 1, KB).astype(jnp.bfloat16)).reshape(
        part_count, 2 * KB**3
    )
    details = jnp.concatenate([candidates, rotations, local_tomo[:, None]], axis=1).astype(
        jnp.float32
    )
    ref_values = references.astype(jnp.float32).reshape(class_count * NSET, 2, KB, KB, KB)
    power = jnp.sum(ref_values * ref_values, axis=(1, 3)).reshape(class_count * NSET, KB * KB)
    quadratic = jnp.dot(power, wedge_rows.T, precision=HIGHEST)
    flat_refs = references.reshape(class_count * NSET, 2 * KB**3)
    slot_spectra, slot_details = (
        lax.all_gather(masked, "cls", axis=0, tiled=True),
        lax.all_gather(details.astype(jnp.bfloat16), "cls", axis=0, tiled=True),
    )
    slot_count = slot_spectra.shape[0]
    inner = lax.dot_general(
        slot_spectra, flat_refs, (((1,), (1,)), ((), ())), preferred_element_type=jnp.float32
    )
    raw_slots, class_hot, rot_hot, tomo_hot = score_slots(
        inner, slot_details, quadratic, class_base, class_count, tomo_count
    )
    raw_own = lax.psum_scatter(raw_slots, "cls", scatter_dimension=0, tiled=True)
    posterior = posterior_weights(raw_own, inverse_noise)
    own_weights = posterior.astype(jnp.bfloat16).reshape(part_count, CAND, ROT)
    slot_weights = lax.all_gather(own_weights, "cls", axis=0, tiled=True)
    coeffs = jnp.einsum(
        "sjc,srn,sjr->cns", class_hot, rot_hot, slot_weights.astype(jnp.float32), precision=HIGHEST
    )
    coeffs = coeffs.reshape(class_count * NSET, slot_count)
    slot_masks = jnp.dot(tomo_hot, wedge_rows, precision=HIGHEST)
    wedge_part = jnp.dot(coeffs, slot_masks, precision=HIGHEST).reshape(class_count, NSET, KB * KB)
    class_part = jnp.dot(
        coeffs.astype(jnp.bfloat16), slot_spectra, preferred_element_type=jnp.float32
    )
    class_part = class_part.reshape(class_count, NSET, 2 * KB**3)
    class_sums, wedge_sums = (
        lax.psum_scatter(class_part, "tomo", scatter_dimension=2, tiled=True),
        lax.psum_scatter(wedge_part, "tomo", scatter_dimension=2, tiled=True),
    )
    return (posterior, class_sums, wedge_sums)


def solution(mesh):
    return jax.shard_map(
        body,
        mesh=mesh,
        in_specs=(
            P(("tomo", "cls"), None, None),
            P(("tomo", "cls")),
            P(("tomo", "cls")),
            P(("tomo", "cls"), None),
            P(("tomo", "cls"), None),
            P("tomo", None, None),
            P("cls", None, None),
        ),
        out_specs=(P(("tomo", "cls"), None), P("cls", None, "tomo"), P("cls", None, "tomo")),
        check_vma=False,
    )
```

profile of v0, /device:TPU:1, one launch (start us, length us, event | category | flops | bytes accessed | tf_op | source)
XLA Modules:
  0.0 484.1 jit_solution(14803889281879913190)
XLA Ops:
  7.2 0.0 all-gather.2.cloned.1.call-start
  7.2 0.0 copy-start.2
  7.2 6.2 %convolution_bitcast_fusion.1 = f32[8,32,4096]{2,1,0:T(8,128)} fusion(bf16[8,64,4096]{2,1,0:T(8,128)(2,1)} %param.7, s32[32]{0:T(128)S(1)} %and_select_fusion), kind=kOutput, calls=%fused_computation.7 | convolution fusion | flops 805337088 | bytes 8388736 | tf_op jit(solution)/shard_map/jn,pnq->pjq/dot_general | solution.py:30
  13.5 0.0 copy-done.2
  13.5 3.6 convolution_bitcast_fusion
  17.1 7.9 %stack.20 = f32[1,8,32,64,64]{4,3,2,1,0:T(8,128)} reshape(f32[8,32,4096]{2,1,0:T(8,128)} %convolution_bitcast_fusion.1) | data formatting | bytes 8388608 | tf_op jit(solution)/shard_map/stack | solution.py:32
  24.9 8.3 %constant_dynamic-update-slice_fusion.1 = f32[2,8,32,64,64]{4,3,2,1,0:T(8,128)} fusion(f32[1,8,32,64,64]{4,3,2,1,0:T(8,128)} %stack.20), kind=kLoop, calls=%fused_computation.75 | loop fusion | bytes 12582912
  33.2 7.9 %stack.21 = f32[1,8,32,64,64]{4,3,2,1,0:T(8,128)} reshape(f32[8,32,4096]{2,1,0:T(8,128)} %convolution_bitcast_fusion) | data formatting | bytes 8388608 | tf_op jit(solution)/shard_map/stack | solution.py:32
  41.0 8.3 %constant_dynamic-update-slice_fusion = f32[2,8,32,64,64]{4,3,2,1,0:T(8,128)} fusion(f32[2,8,32,64,64]{4,3,2,1,0:T(8,128)} %constant_dynamic-update-slice_fusion.1, f32[1,8,32,64,64]{4,3,2,1,0:T(8,128)} %stack.21), kind=kLoop, calls=%fused_computation.74 | loop fusion | bytes 16777216 | tf_op jit(solution)/shard_map/stack | solution.py:32
  49.3 15.9 %convolution_bitcast_fusion.2 = f32[2,8,32,32,64]{4,3,2,1,0:T(8,128)} fusion(f32[2,8,32,64,64]{4,3,2,1,0:T(8,128)} %constant_dynamic-update-slice_fusion, s32[32]{0:T(128)S(1)} %and_select_fusion), kind=kOutput, calls=%fused_computation.15 | convolution fusion | flops 805339136 | bytes 12583040 | tf_op jit(solution)/shard_map/kn,apjnz->apjkz/dot_general | solution.py:34
  65.2 0.0 copy-done
  65.2 12.3 %convolution_bitcast_fusion.3 = f32[2,8,32,32,64]{4,3,2,1,0:T(8,128)} fusion(f32[2,8,32,64,64]{4,3,2,1,0:T(8,128)S(1)} %copy-done, s32[32]{0:T(128)S(1)} %and_select_fusion), kind=kOutput, calls=%fused_computation.16 | convolution fusion | flops 805337088 | bytes 12583040 | tf_op jit(solution)/shard_map/kn,apjnz->apjkz/dot_general | solution.py:33
  77.5 9.9 %slice_subtract_fusion.1 = (f32[1,8,32,32,64]{4,3,2,1,0:T(8,128)S(1)}, f32[1,8,32,32,64]{4,3,2,1,0:T(8,128)}) fusion(f32[2,8,32,32,64]{4,3,2,1,0:T(8,128)} %convolution_bitcast_fusion.2, f32[2,8,32,32,64]{4,3,2,1,0:T(8,128)} %convolution_bitcast_fusion.3), kind=kLoop, calls=%fused_computation.13 | loop fusion | flops 1048576 | bytes 12582912 | tf_op jit(solution)/shard_map/sub | solution.py:35
  87.4 10.6 %fusion.2 = f32[2,8,32,32,32]{4,3,2,1,0:T(8,128)} fusion(f32[1,8,32,32,64]{4,3,2,1,0:T(8,128)} %get-tuple-element.8, f32[1,8,32,32,64]{4,3,2,1,0:T(8,128)S(1)} %get-tuple-element.7, s32[32]{0:T(128)S(1)} %and_select_fusion), kind=kOutput, calls=%fused_computation.4 | convolution fusion | flops 403734528 | bytes 6291584 | tf_op jit(solution)/shard_map/apjkn,ln->apjkl/dot_general | solution.py:37
  98.0 9.5 %fusion.3 = f32[2,8,32,32,32]{4,3,2,1,0:T(8,128)} fusion(f32[1,8,32,32,64]{4,3,2,1,0:T(8,128)S(1)} %copy-done.1, f32[1,8,32,32,64]{4,3,2,1,0:T(8,128)S(1)} %get-tuple-element.7, s32[32]{0:T(128)S(1)} %and_select_fusion), kind=kOutput, calls=%fused_computation.5 | convolution fusion | flops 403732480 | bytes 6291584 | tf_op jit(solution)/shard_map/apjkn,ln->apjkl/dot_general | solution.py:36
  107.6 0.0 copy-done.3
  107.6 0.1 convert_element_type.58
  107.7 0.1 dot_general.62
  107.8 0.3 convolution_convert_fusion
  108.1 6.9 %fusion.6 = (bf16[8,1,32,32,32]{4,3,2,0,1:T(8,128)(2,1)S(1)}, bf16[8,1,32,32,32]{4,3,2,0,1:T(8,128)(2,1)S(1)}) fusion(f32[2,8,32,32,32]{4,3,2,1,0:T(8,128)} %fusion.2, f32[2,8,32,32,32]{4,3,2,1,0:T(8,128)} %fusion.3), kind=kLoop, calls=%fused_computation.17 | loop fusion | flops 1048576 | bytes 5242880 | tf_op jit(solution)/shard_map/sub | solution.py:38
  115.0 1.2 maximum_multiply_fusion
  116.2 3.0 copy.50
  119.2 7.6 %mul.130 = bf16[8,65536]{1,0:T(8,128)(2,1)} reshape(bf16[8,2,32,32,32]{4,3,2,1,0:T(8,128)(2,1)} %copy.50) | data formatting | bytes 2097152 | tf_op jit(solution)/shard_map/mul | solution.py:81
  126.8 0.0 all-gather.2.cloned.1.call-update
  126.8 0.2 reduce-scatter.7.cloned.1.call-start
  127.0 10.3 %convert_multiply_fusion = f32[4,16,65536]{2,1,0:T(8,128)} fusion(bf16[4,16,65536]{2,1,0:T(8,128)(2,1)} %param.13), kind=kLoop, calls=%fused_computation | loop fusion | flops 8388608 | bytes 25165824 | tf_op jit(solution)/shard_map/mul | solution.py:88
  137.3 60.6 %mul.132 = f32[64,2,32,32,32]{4,3,2,1,0:T(8,128)} reshape(f32[4,16,65536]{2,1,0:T(8,128)} %convert_multiply_fusion) | data formatting | bytes 33554432 | tf_op jit(solution)/shard_map/mul | solution.py:88
  197.9 0.1 copy.47
  198.0 0.1 copy.46
  198.1 0.1 fusion.53
  198.2 13.4 %all_gather.9 = bf16[64,13]{1,0:T(8,128)(2,1)S(1)} all-gather(bf16[8,13]{1,0:T(8,128)(2,1)S(1)} %fusion.53), channel_id=1, replica_groups=mesh['tomo'=16,'cls'=8] {'cls'}, dimensions={0}, use_global_device_ids=true | all-gather | bytes 1872 | tf_op jit(solution)/shard_map/all_gather | solution.py:93
  211.6 0.1 slice.54
  211.7 21.2 %reduce_sum.18 = f32[64,32,32]{2,1,0:T(8,128)S(1)} reduce(f32[64,2,32,32,32]{4,3,2,1,0:T(8,128)} %mul.132, f32[]{:T(128)} %constant.45.clone.1), dimensions={1,3}, to_apply=%region_0.1 | reduce | flops 4128768 | bytes 17039364 | tf_op jit(solution)/shard_map/reduce_sum | solution.py:88
  232.8 0.6 dynamic-slice
  234.1 0.2 slice_reduce_fusion
  234.3 0.3 convolution_bitcast_fusion.4
  234.6 1.5 convolution_bitcast_fusion.5
  236.1 8.1 %fusion.93 = f32[64,64]{1,0:T(8,128)S(1)} fusion(bf16[64,65536]{1,0:T(8,128)(2,1)} %all-gather.2.cloned.1.call-done, bf16[64,65536]{1,0:T(8,128)(2,1)} %bitcast.82), kind=kOutput, calls=%fused_computation.122 | convolution fusion | flops 536870912 | bytes 16793600 | tf_op jit(solution)/shard_map/dot_general | solution.py:96
  244.2 0.2 fusion.8
  244.4 0.1 copy.53
  244.5 0.1 copy.54
  244.6 0.4 fusion.11
  245.0 0.5 fusion.14
  245.5 23.1 %all-reduce = f32[64,4,8]{2,1,0:T(4,128)S(1)} all-reduce(f32[64,4,8]{2,1,0:T(4,128)S(1)} %fusion.14), channel_id=2, replica_groups=mesh['tomo'=16,'cls'=8] {'cls'}, use_global_device_ids=true, to_apply=%region_1.2.clone | all-reduce | flops 2048 | bytes 16384
  268.7 0.2 multiply_reduce_fusion
  268.9 0.2 fusion.40
  269.1 0.1 divide_convert_fusion
  269.2 16.4 %all_gather.11 = bf16[64,4,8]{2,1,0:T(4,128)(2,1)S(1)} all-gather(bf16[8,4,8]{2,1,0:T(4,128)(2,1)S(1)} %divide_convert_fusion), channel_id=1, replica_groups=mesh['tomo'=16,'cls'=8] {'cls'}, dimensions={0}, use_global_device_ids=true | all-gather | bytes 4608 | tf_op jit(solution)/shard_map/all_gather | solution.py:105
  285.6 0.3 fusion.12
  285.9 0.4 fusion.10
  286.3 0.1 copy.56
  286.4 0.4 fusion.24
  286.8 0.8 copy.60
  287.6 1.7 reshape.142
  289.3 0.0 reduce-scatter.7.cloned.1.call-update
  289.3 0.0 reduce-scatter.5.cloned.1.call-start
  289.4 11.4 %fusion = f32[4,16,65536]{2,1,0:T(8,128)} fusion(bf16[64,65536]{1,0:T(8,128)(2,1)} %all-gather.2.cloned.1.call-done, f32[64,4,16]{0,2,1:T(8,128)S(1)} %copy.56), kind=kOutput, calls=%fused_computation.2 | convolution fusion | flops 536870912 | bytes 25182208 | tf_op jit(solution)/shard_map/dot_general | solution.py:112
  300.8 0.0 reduce-scatter.5.cloned.1.call-update
  300.8 0.1 reshape.133
  300.9 0.7 exponential_divide_fusion
  301.6 60.3 %reduce-scatter.7.cloned.1.call-done = f32[64,64]{1,0:T(8,128)} async-done(((f32[1024,64]{1,0:T(8,128)}), f32[64,64]{1,0:T(8,128)}) %reduce-scatter.7.cloned.1.call-update) | async-done | bytes 16400
  361.9 0.9 reshape.143
  362.7 0.7 copy.61
  363.4 113.9 %reduce-scatter.5.cloned.1.call-done = f32[4,16,4096]{2,1,0:T(8,128)} async-done(((f32[4,16,65536]{2,1,0:T(8,128)}), f32[4,16,4096]{2,1,0:T(8,128)}) %reduce-scatter.5.cloned.1.call-update) | async-done | bytes 1048592 | tf_op jit(solution)/shard_map/reduce_scatter | solution.py:117
  (22 shorter events, 0.1 us)
Async XLA Ops:
  7.2 228.9 %all-gather.2.cloned.1.call-start = ((), (), s32[]{:S(2)}) async-start(), calls=%async_computation.2 | async-start | bytes 9437184 | tf_op jit(solution)/shard_map/all_gather | solution.py:92
  7.2 6.3 %copy-start.2 = (bf16[8,64,4096]{2,1,0:T(8,128)(2,1)S(1)}, bf16[8,64,4096]{2,1,0:T(8,128)(2,1)}, u32[]{:S(2)}) copy-start(bf16[8,64,4096]{2,1,0:T(8,128)(2,1)} %param.7) | copy-start | bytes 12582916
  49.3 15.9 %copy-start = (f32[2,8,32,64,64]{4,3,2,1,0:T(8,128)S(1)}, f32[2,8,32,64,64]{4,3,2,1,0:T(8,128)}, u32[]{:S(2)}) copy-start(f32[2,8,32,64,64]{4,3,2,1,0:T(8,128)} %constant_dynamic-update-slice_fusion) | copy-start | bytes 25165828
  87.4 10.6 %copy-start.1 = (f32[1,8,32,32,64]{4,3,2,1,0:T(8,128)S(1)}, f32[1,8,32,32,64]{4,3,2,1,0:T(8,128)}, u32[]{:S(2)}) copy-start(f32[1,8,32,32,64]{4,3,2,1,0:T(8,128)} %get-tuple-element.8) | copy-start | bytes 6291460
  98.0 9.6 %copy-start.3 = (s32[4,32,32]{2,1,0:T(8,128)S(1)}, s32[4,32,32]{2,1,0:T(8,128)}, u32[]{:S(2)}) copy-start(s32[4,32,32]{2,1,0:T(8,128)} %param.12) | copy-start | bytes 49156
  98.0 9.8 %copy-start.7 = (s32[8]{0:T(128)S(1)}, s32[8]{0:T(128)}, u32[]{:S(2)}) copy-start(s32[8]{0:T(128)} %param.9) | copy-start | bytes 100
  126.8 235.1 %reduce-scatter.7.cloned.1.call-start = ((), (), s32[]{:S(2)}) async-start(), calls=%async_computation.4 | async-start | bytes 557056
  137.3 60.7 %copy-start.6 = (s32[8,4]{0,1:T(4,128)S(1)}, s32[8,4]{0,1:T(4,128)}, u32[]{:S(2)}) copy-start(s32[8,4]{0,1:T(4,128)} %param.10) | copy-start | bytes 388
  137.3 60.8 %copy-start.5 = (s32[8,8]{1,0:T(8,128)S(1)}, s32[8,8]{1,0:T(8,128)}, u32[]{:S(2)}) copy-start(s32[8,8]{1,0:T(8,128)} %param.11) | copy-start | bytes 772
  211.7 21.2 %copy-start.8 = (u32[128]{0:T(128)S(1)}, u32[128]{0:T(128)}, u32[]{:S(2)}) copy-start(u32[128]{0:T(128)} %constant.57) | copy-start | bytes 1540
  236.1 32.6 %copy-start.4 = (f32[8]{0:T(128)S(1)}, f32[8]{0:T(128)}, u32[]{:S(2)}) copy-start(f32[8]{0:T(128)} %param.8) | copy-start | bytes 100
  289.3 188.1 %reduce-scatter.5.cloned.1.call-start = ((), (), s32[]{:S(2)}) async-start(), calls=%async_computation.3 | async-start | bytes 17825792 | tf_op jit(solution)/shard_map/reduce_scatter | solution.py:117
Sparse Core Ops, SparseCore 0:
  126.9 53.2 all-gather.1
  289.4 72.3 reduce-scatter.6
  365.8 111.4 reduce-scatter.4
where the time goes:
time: 493 us; the launch traced here: 484 us
  waiting for transfers between devices  174 us (35%)
  local copies, waits for them, and re-layouts  109 us (22%)
  matrix products  81.9 us (17%)
  blocking collectives  52.9 us (11%)
  other arithmetic  50.8 us (10%)
  between operations  14.8 us (3%)
    reduce_scatter x1, waiting for transfers between devices, body(): lax.psum_scatter(class_part, 'tomo', scatter_dimension=2, tiled=True)  114 us
    mul x1, local copies, waits for them, and re-layouts, body(): ref_values * ref_values  60.6 us
    unnamed x4, waiting for transfers between devices  60.3 us
    another operation x3, local copies, waits for them, and re-layouts, band_spectra(): jnp.stack([first_re, first_im]).reshape(2, volume_count, KB, length, length)  24 us
    unnamed x1, blocking collectives  23.1 us
    reduce_sum x1, other arithmetic, body(): jnp.sum(ref_values * ref_values, axis=(1, 3))  21.2 us
    all_gather x1, blocking collectives, body(): slot_weights = lax.all_gather(own_weights, 'cls', axis=0, tiled=True)  16.4 us
    dot_general x1, matrix products, band_spectra(): sin_part = jnp.einsum('kn,apjnz->apjkz', sine, stacked, precision=HIGHEST)  15.9 us
  transfers between devices with their start and end apart: 3, of which 2 were waited for; matrix products, arithmetic and copies ran while one was open for 22% of the time, Pallas kernels for 0%

commit v1 on v0

v1 whole, which is shorter than its diff:
```python
import math

import jax
import jax.numpy as jnp
import numpy as np
from jax import lax
from jax.experimental import pallas as pl
from jax.experimental.pallas import tpu as pltpu
from jax.sharding import PartitionSpec as P


VOX = 64
KB = 32
NSET = 16
ROT = 8
CAND = 4
PART = 8
ROWS = 16
COLS = 8
CLS_DEV = 4
SLICE = 2 * KB**3 // ROWS
EXTRA = 256
WIDTH = SLICE + EXTRA
HALF = WIDTH // 2
CODE_AT = 192


def split_table(table):
    high = table.astype(jnp.bfloat16)
    low = (table - np.asarray(high, np.float32)).astype(jnp.bfloat16)
    return high, low


def dft_constants():
    frequency = np.arange(KB) - KB // 2
    residue = (frequency[:, None] * np.arange(VOX)[None, :]) % VOX
    radians = residue * (2.0 * math.pi / VOX)
    both = (np.stack([np.cos(radians), -np.sin(radians)]) / math.sqrt(VOX)).astype(np.float32)
    depth_table = np.kron(np.eye(4, dtype=np.float32), both.reshape(2 * KB, VOX))
    wz = np.concatenate(split_table(depth_table), axis=0)
    wide = np.einsum("akx,pq->pxakq", both, np.eye(PART, dtype=np.float32))
    wxh, wxl = split_table(wide.reshape(PART * VOX, 2 * KB * PART))
    high, low = split_table(both.reshape(2 * KB, VOX))
    wy = np.concatenate([high, high, low], axis=1)
    return wz, wxh, wxl, wy


def dft_kernel(p_ref, wz_ref, wxh_ref, wxl_ref, wy_ref, mask_ref, ext_ref, out_ref, mid, last):
    step = pl.program_id(0)
    data = p_ref[...].reshape(PART * VOX, 4 * VOX)
    first = lax.dot_general(
        wz_ref[...], data, (((1,), (1,)), ((), ())), preferred_element_type=jnp.float32
    )
    first = first[: 8 * KB] + first[8 * KB :]
    high = first.astype(jnp.bfloat16)
    low = (first - high.astype(jnp.float32)).astype(jnp.bfloat16)
    second = (
        jnp.dot(high, wxh_ref[...], preferred_element_type=jnp.float32)
        + jnp.dot(low, wxh_ref[...], preferred_element_type=jnp.float32)
        + jnp.dot(high, wxl_ref[...], preferred_element_type=jnp.float32)
    )
    for yy in range(4):
        cos_rows = second[yy * 64 : yy * 64 + 32]
        sin_rows = second[yy * 64 + 32 : yy * 64 + 64]
        real = cos_rows[:, :256] - sin_rows[:, 256:]
        imag = sin_rows[:, :256] + cos_rows[:, 256:]
        rows = pl.ds(pl.multiple_of((step * 4 + yy) * KB, KB), KB)
        mid[0, rows, :] = real[:, :128]
        mid[1, rows, :] = real[:, 128:]
        mid[2, rows, :] = imag[:, :128]
        mid[3, rows, :] = imag[:, 128:]

    @pl.when(step == pl.num_programs(0) - 1)
    def _():
        for kz in range(KB):
            values = jnp.concatenate(
                [mid[block, pl.ds(kz, VOX, stride=KB), :] for block in range(4)], axis=1
            )
            top = values.astype(jnp.bfloat16)
            rest = (values - top.astype(jnp.float32)).astype(jnp.bfloat16)
            third = jnp.dot(
                wy_ref[...],
                jnp.concatenate([top, rest, top], axis=0),
                preferred_element_type=jnp.float32,
            )
            real = third[:KB, :256] - third[KB:, 256:]
            imag = third[KB:, :256] + third[:KB, 256:]
            rows = pl.ds(kz, KB, stride=KB)
            last[0, rows, :] = real[:, :128]
            last[1, rows, :] = real[:, 128:]
            last[2, rows, :] = imag[:, :128]
            last[3, rows, :] = imag[:, 128:]
        for block in range(4):
            turned = last[block].T
            for k in range(16):
                kx = (block % 2) * 16 + k
                target = (block // 2) * 8 + kx // 4
                keep = jnp.concatenate([mask_ref[kx]] * 8, axis=1)
                piece = turned[k * PART : (k + 1) * PART, :] * keep
                out_ref[target, :, (kx % 4) * 1024 : (kx % 4 + 1) * 1024] = piece.astype(
                    jnp.bfloat16
                )
        out_ref[:, :, SLICE:] = ext_ref[...]


def spectra_call(particles, mask_tiles, extras):
    wz, wxh, wxl, wy = dft_constants()
    whole = lambda shape: pl.BlockSpec(shape, lambda i: (0,) * len(shape))
    return pl.pallas_call(
        dft_kernel,
        grid=(16,),
        in_specs=[
            pl.BlockSpec((PART, VOX, 256), lambda i: (0, 0, i)),
            whole(wz.shape),
            whole(wxh.shape),
            whole(wxl.shape),
            whole(wy.shape),
            whole((KB, PART, 128)),
            whole((ROWS, PART, EXTRA)),
        ],
        out_specs=whole((ROWS, PART, WIDTH)),
        out_shape=jax.ShapeDtypeStruct((ROWS, PART, WIDTH), jnp.bfloat16),
        scratch_shapes=[
            pltpu.VMEM((4, VOX * KB, 128), jnp.float32),
            pltpu.VMEM((4, KB * KB, 128), jnp.float32),
        ],
        compiler_params=pltpu.CompilerParams(dimension_semantics=("arbitrary",)),
        cost_estimate=pl.CostEstimate(
            flops=20_000_000_000, bytes_accessed=8_000_000, transcendentals=0
        ),
        name="dft",
    )(particles, *(jnp.asarray(t) for t in (wz, wxh, wxl, wy)), mask_tiles, extras)


def score_kernel(base_ref, slots_ref, noise_ref, *refs):
    pieces, out_ref, codes_ref = refs[:-2], refs[-2], refs[-1]
    slots = slots_ref[:, :SLICE]
    codes = slots_ref[:, SLICE + 128 :].astype(jnp.float32).T[CODE_AT - 128 : CODE_AT - 128 + 16]
    codes_ref[...] = codes
    row = lax.broadcasted_iota(jnp.int32, (128, 512), 0)
    col = lax.broadcasted_iota(jnp.int32, (128, 512), 1)
    spread = ((row // KB == col // 128) & (row % KB == col % KB)).astype(jnp.bfloat16)
    keep = jnp.dot(
        slots_ref[:, SLICE : SLICE + 128], spread, preferred_element_type=jnp.float32
    ).astype(jnp.bfloat16)
    chosen = [jnp.zeros((NSET, 128), jnp.float32) for _ in range(CAND)]
    contract = (((1,), (1,)), ((), ()))
    for index, (slot, offset) in enumerate(PIECES):
        ref = pieces[index]
        count = ref.shape[0]
        inner = lax.dot_general(ref[...], slots, contract, preferred_element_type=jnp.float32)
        sums = []
        for k in range(4):
            total = jnp.zeros((count, 128), jnp.float32)
            for j in range(8):
                at = k * 1024 + j * 128
                value = ref[:, at : at + 128].astype(jnp.float32)
                total = total + value * value
            sums.append(total)
        power = jnp.concatenate(sums, axis=1)
        one = power.astype(jnp.bfloat16)
        left = power - one.astype(jnp.float32)
        two = left.astype(jnp.bfloat16)
        three = (left - two.astype(jnp.float32)).astype(jnp.bfloat16)
        stacked = jnp.concatenate([one, two, three], axis=0)
        penalty = lax.dot_general(stacked, keep, contract, preferred_element_type=jnp.float32)
        penalty = (penalty[2 * count :] + penalty[count : 2 * count]) + penalty[:count]
        table = inner - 0.5 * penalty
        for local in range(count // NSET):
            label = (base_ref[slot] * CLS_DEV + offset + local).astype(jnp.float32)
            block = table[local * NSET : (local + 1) * NSET]
            for j in range(CAND):
                chosen[j] = chosen[j] + jnp.where(codes[j : j + 1] == label, block, 0.0)
    copies = lax.broadcasted_iota(jnp.int32, (NSET, 128), 0).astype(jnp.float32)
    for r in range(ROT):
        hit = codes[CAND + r : CAND + r + 1] == copies
        for j in range(CAND):
            out_ref[j * ROT + r : j * ROT + r + 1, :] = jnp.sum(
                jnp.where(hit, chosen[j], 0.0), axis=0, keepdims=True
            )
    out_ref[CAND * ROT :, :] = noise_ref[...]


PIECES = ((0, 0), (1, 0), (2, 0), (3, 0), (3, 2), (4, 0), (5, 0), (6, 0), (7, 0), (7, 2))


def score_call(bases, slots, noise_rows, pieces):
    vmem = pl.BlockSpec(memory_space=pltpu.VMEM)
    return pl.pallas_call(
        score_kernel,
        in_specs=[pl.BlockSpec(memory_space=pltpu.SMEM)] + [vmem] * (2 + len(pieces)),
        out_specs=(vmem, vmem),
        out_shape=(
            jax.ShapeDtypeStruct((CAND * ROT + 8, 128), jnp.float32),
            jax.ShapeDtypeStruct((16, 128), jnp.float32),
        ),
        cost_estimate=pl.CostEstimate(
            flops=1_000_000_000, bytes_accessed=6_000_000, transcendentals=0
        ),
        name="score",
    )(bases, slots, noise_rows, *pieces)


def softmax_kernel(at_ref, parts_ref, codes_ref, post_ref, coef_ref, turned):
    total = parts_ref[0]
    for row in range(1, ROWS):
        total = total + parts_ref[row]
    logits = total[CAND * ROT : CAND * ROT + 1] * total[: CAND * ROT]
    peak = jnp.max(logits, axis=0, keepdims=True)
    weight = jnp.exp(logits - peak)
    posterior = weight / jnp.sum(weight, axis=0, keepdims=True)
    padded = jnp.concatenate([posterior, jnp.zeros((96, 128), jnp.float32)], axis=0)
    turned[...] = padded.T
    own = turned[pl.ds(pl.multiple_of(at_ref[0] * PART, PART), PART), :]
    post_ref[...] = own[:, : CAND * ROT]
    rounded = posterior.astype(jnp.bfloat16).astype(jnp.float32)
    codes = codes_ref[...]
    copies = lax.broadcasted_iota(jnp.int32, (NSET, 128), 0).astype(jnp.float32)
    spread = []
    for j in range(CAND):
        value = jnp.zeros((NSET, 128), jnp.float32)
        for r in range(ROT):
            hit = codes[CAND + r : CAND + r + 1] == copies
            value = value + jnp.where(hit, rounded[j * ROT + r : j * ROT + r + 1], 0.0)
        spread.append(value)
    for label in range(COLS * CLS_DEV):
        value = jnp.zeros((NSET, 128), jnp.float32)
        for j in range(CAND):
            value = value + jnp.where(codes[j : j + 1] == float(label), spread[j], 0.0)
        at = (label % CLS_DEV) * NSET
        coef_ref[label // CLS_DEV, at : at + NSET, :] = value.astype(jnp.bfloat16)


def softmax_call(row_index, parts, codes):
    vmem = pl.BlockSpec(memory_space=pltpu.VMEM)
    return pl.pallas_call(
        softmax_kernel,
        in_specs=[pl.BlockSpec(memory_space=pltpu.SMEM), vmem, vmem],
        out_specs=(vmem, vmem),
        out_shape=(
            jax.ShapeDtypeStruct((PART, CAND * ROT), jnp.float32),
            jax.ShapeDtypeStruct((COLS, CLS_DEV * NSET, 128), jnp.bfloat16),
        ),
        scratch_shapes=[pltpu.VMEM((128, 128), jnp.float32)],
        name="weights",
    )(row_index, parts, codes)


def sums_kernel(base_ref, coef_ref, *refs):
    pieces, class_ref, wedge_ref = refs[:-2], refs[-2], refs[-1]
    coefs = [coef_ref[base_ref[slot]] for slot in range(8)]
    start = 0
    for stop in (HALF, WIDTH):
        second = start > 0
        picks = ((0, 0), (1, 1), (2, 2), (3, 4 if second else 3))
        picks = picks + ((4, 5), (5, 6), (6, 7), (7, 9 if second else 8))
        total = None
        for slot, index in picks:
            ref = pieces[index]
            block = ref[:, start:stop] if ref.shape[1] == WIDTH else ref[...]
            term = jnp.dot(coefs[slot], block, preferred_element_type=jnp.float32)
            total = term if total is None else total + term
        if second:
            class_ref[:, start:] = total[:, : SLICE - start]
            at = SLICE + 128 - start
            wedge_ref[...] = total[:, at : at + 64]
        else:
            class_ref[:, :stop] = total
        start = stop


def sums_call(bases, coefs, pieces):
    vmem = pl.BlockSpec(memory_space=pltpu.VMEM)
    return pl.pallas_call(
        sums_kernel,
        in_specs=[pl.BlockSpec(memory_space=pltpu.SMEM)] + [vmem] * (1 + len(pieces)),
        out_specs=(vmem, vmem),
        out_shape=(
            jax.ShapeDtypeStruct((CLS_DEV * NSET, SLICE), jnp.float32),
            jax.ShapeDtypeStruct((CLS_DEV * NSET, 64), jnp.float32),
        ),
        name="sums",
    )(bases, coefs, *pieces)


def along_x(value, hops):
    pairs = [(i, ((i // 2 + hops) % 4) * 2 + i % 2) for i in range(COLS)]
    return lax.ppermute(value, "cls", pairs)


def other_core(value):
    return lax.ppermute(value, "cls", [(i, i ^ 1) for i in range(COLS)])


def around(value, first_half, second_half):
    ahead = along_x(value, 1)
    behind = along_x(value, -1)
    other = other_core(value)
    far_one = along_x(first_half(ahead), 1)
    far_two = along_x(second_half(behind), -1)
    other_near = [other_core(ahead), other_core(behind)]
    other_far = [other_core(far_one), other_core(far_two)]
    return [value, ahead, behind, far_one, far_two, other] + other_near + other_far


def inner(particles, inverse_noise, tomogram, candidates, rotations, wedge, references):
    row = lax.axis_index("tomo")
    col = lax.axis_index("cls")
    x, core = col >> 1, col & 1
    bases = jnp.stack(
        [((x + dx) & 3) * 2 + (core ^ k) for k in (0, 1) for dx in (0, 3, 1, 2)]
    ).astype(jnp.int32)

    flat_refs = references.reshape(CLS_DEV * NSET, 2 * KB**3)
    ref_slice = lax.dynamic_slice(flat_refs, (0, row * SLICE), (CLS_DEV * NSET, SLICE))
    ref_pieces = around(ref_slice, lambda v: v[:32], lambda v: v[32:])

    local = tomogram - row * wedge.shape[0]
    wedge_rows = wedge.reshape(wedge.shape[0], KB * KB)
    masks = jnp.zeros((PART, KB * KB), jnp.int32)
    for index in range(wedge.shape[0]):
        masks = jnp.where((local == index)[:, None], wedge_rows[index][None, :], masks)
    masks = masks.astype(jnp.float32)
    mask_tiles = jnp.tile(masks.reshape(PART, KB, KB).transpose(1, 0, 2), (1, 1, 4))
    planes = masks.reshape(PART, 8, 128).transpose(1, 0, 2)
    entries = masks.reshape(PART, ROWS, 64).transpose(1, 0, 2)
    codes = jnp.concatenate([candidates, rotations], axis=1).astype(jnp.float32)
    codes = jnp.pad(codes, ((0, 0), (0, 64 - CAND - ROT)))
    extras = jnp.concatenate(
        [
            jnp.concatenate([planes, planes], axis=0),
            entries,
            jnp.broadcast_to(codes[None], (ROWS, PART, 64)),
        ],
        axis=2,
    ).astype(jnp.bfloat16)
    spectra = spectra_call(particles, mask_tiles, extras)
    slots = lax.all_to_all(spectra, "tomo", 0, 0, tiled=True).reshape(ROWS * PART, WIDTH)
    slot_pieces = around(slots, lambda v: v[:, :HALF], lambda v: v[:, HALF:])

    lane = jnp.arange(128, dtype=jnp.int32)
    noise_row = jnp.where(lane // PART == row, jnp.tile(inverse_noise, ROWS), 0.0)
    noise_rows = jnp.broadcast_to(noise_row[None], (8, 128))
    partial, codes_turned = score_call(bases, slots, noise_rows, ref_pieces)
    copies = jnp.broadcast_to(partial[None], (ROWS,) + partial.shape)
    parts = lax.all_to_all(copies, "tomo", 0, 0, tiled=True)
    posterior, coefs = softmax_call(row.astype(jnp.int32)[None], parts, codes_turned)
    coefs = lax.all_to_all(coefs, "cls", 0, 0, tiled=True)
    class_sums, wedge_sums = sums_call(bases, coefs, slot_pieces)
    return (
        posterior,
        class_sums.reshape(CLS_DEV, NSET, SLICE),
        wedge_sums.reshape(CLS_DEV, NSET, 64),
    )


def solution(mesh):
    return jax.shard_map(
        inner,
        mesh=mesh,
        in_specs=(
            P(("tomo", "cls"), None, None),
            P(("tomo", "cls")),
            P(("tomo", "cls")),
            P(("tomo", "cls"), None),
            P(("tomo", "cls"), None),
            P("tomo", None, None),
            P("cls", None, None),
        ),
        out_specs=(P(("tomo", "cls"), None), P("cls", None, "tomo"), P("cls", None, "tomo")),
        check_vma=False,
    )
```

time: 493 us -> 166 us (0.34); the launches traced: 484 us -> 165 us
  waiting for transfers between devices: 174 us -> 55.9 us
  local copies, waits for them, and re-layouts: 109 us -> 8.61 us
  matrix products: 81.9 us -> 0 us
  other arithmetic: 50.8 us -> 2.41 us
  Pallas kernels: 0 us -> 39.6 us
  starting transfers between devices: 0.29 us -> 34.6 us
  blocking collectives: 52.9 us -> 23.2 us
  between operations: 14.8 us -> 0.82 us
    reduce_scatter x1 -> x0, waiting for transfers between devices: 114 us -> none  [body(): lax.psum_scatter(class_part, 'tomo', scatter_dimension=2, tiled=True)]
    dot_general x17 -> x0, matrix products: 81.9 us -> none  [the longest x1 15.9 us: band_spectra(): sin_part = jnp.einsum('kn,apjnz->apjkz', sine, stacked, precision=HIGHEST)]
    mul x3 -> x0, local copies, waits for them, and re-layouts: 71.1 us -> none  [the longest x1 60.6 us: body(): ref_values * ref_values]
    unnamed x4 -> x0, waiting for transfers between devices: 60.3 us -> none
    ppermute x0 -> x18, waiting for transfers between devices: none -> 39.6 us  [the longest x8 39.6 us: along_x(): return lax.ppermute(value, 'cls', pairs)]
    pallas_call x0 -> x4, Pallas kernels: none -> 39.6 us  [the longest x1 24.9 us: spectra_call(): pl.pallas_call(dft_kernel, grid=(16,), in_specs=[pl.BlockSpec((PART, VOX,...]
    all_gather x2 -> x0, blocking collectives: 29.8 us -> none  [the longest x1 16.4 us: body(): slot_weights = lax.all_gather(own_weights, 'cls', axis=0, tiled=True)]
    ppermute x0 -> x18, starting transfers between devices: none -> 26 us  [the longest x10 15.7 us: other_core(): return lax.ppermute(value, 'cls', [(i, i ^ 1) for i in range(COLS)])]
  transfers between devices with their start and end apart: 3 -> 19, of which waited for: 2 -> 4; matrix products, arithmetic and copies ran while one was open for 22% -> 3% of each run, Pallas kernels for 0% -> 5%
where the time goes in v1:
time: 166 us; the launch traced here: 165 us
  waiting for transfers between devices  55.9 us (34%)
  Pallas kernels  39.6 us (24%)
  starting transfers between devices  34.6 us (21%)
  blocking collectives  23.2 us (14%)
  local copies, waits for them, and re-layouts  8.61 us (5%)
  other arithmetic  2.41 us (1%)
    ppermute x8, waiting for transfers between devices, along_x(): return lax.ppermute(value, 'cls', pairs)  39.6 us
    pallas_call x1, Pallas kernels, spectra_call(): pl.pallas_call(dft_kernel, grid=(16,), in_specs=[pl.BlockSpec((PART, VOX,...  24.9 us
    all_to_all x1, waiting for transfers between devices, inner(): lax.all_to_all(spectra, 'tomo', 0, 0, tiled=True)  16.4 us
    ppermute x10, starting transfers between devices, other_core(): return lax.ppermute(value, 'cls', [(i, i ^ 1) for i in range(COLS)])  15.7 us
    all_to_all x1, blocking collectives, inner(): parts = lax.all_to_all(copies, 'tomo', 0, 0, tiled=True)  12.2 us
    all_to_all x1, blocking collectives, inner(): coefs = lax.all_to_all(coefs, 'cls', 0, 0, tiled=True)  11 us
    ppermute x8, starting transfers between devices, along_x(): return lax.ppermute(value, 'cls', pairs)  10.3 us
    all_to_all x1, starting transfers between devices, inner(): lax.all_to_all(spectra, 'tomo', 0, 0, tiled=True)  8.59 us
  transfers between devices with their start and end apart: 19, of which 4 were waited for; matrix products, arithmetic and copies ran while one was open for 3% of the time, Pallas kernels for 5%

profile of v1, /device:TPU:1, one launch (start us, length us, event | category | flops | bytes accessed | tf_op | source)
XLA Modules:
  0.0 165.2 jit_solution(808359837718848994)
XLA Ops:
  0.6 0.8 fusion
  1.4 0.1 broadcast_in_dim.153
  1.5 0.1 broadcast_in_dim.166
  1.6 0.1 broadcast_in_dim.156
  1.6 0.1 broadcast_in_dim.169
  1.7 0.1 broadcast_in_dim.162
  1.8 0.1 broadcast_in_dim.175
  1.8 0.1 broadcast_in_dim.159
  1.9 0.1 broadcast_in_dim.172
  2.0 0.7 broadcast_compare_fusion.3
  2.7 0.8 copy.15
  3.4 0.8 add_convert_fusion
  4.2 0.1 select_convert_fusion
  4.3 0.1 tile.8
  4.4 0.9 tile.9.mask_ref
  5.4 0.1 convert_convert_fusion
  5.4 0.1 convert_convert_fusion.1
  5.5 0.7 pad_maximum_fusion.ext_ref
  6.2 24.9 %dft.1 = bf16[16,8,4352]{2,1,0:T(8,128)(2,1)} custom-call(bf16[8,64,4096]{2,1,0:T(8,128)(2,1)} %p_ref.1, bf16[512,256]{1,0:T(8,128)(2,1)} %constant.54.clone.wz_ref, bf16[512,512]{1,0:T(8,128)(2,1)} %constant.55.clone.wxh_ref, bf16[512,512]{1,0:T(8,128)(2,1)} %constant.56.clone.wxl_ref, bf16[64,192]{1,0:T(8,128)(2,1)} %constant.57.clone.wy_ref, ...), custom_call_target="tpu_custom_call" | custom-call | flops 20000000000 | bytes 8000000 | tf_op jit(solution)/shard_map/dft/pallas_call | solution.py:109
  31.2 8.6 %all-to-all-start = ((bf16[16,8,4352]{2,1,0:T(8,128)(2,1)}), bf16[16,8,4352]{2,1,0:T(8,128)(2,1)S(1)}, u32[]{:S(2)}, u32[]{:S(2)}) async-start(bf16[16,8,4352]{2,1,0:T(8,128)(2,1)} %dft.1), calls=%async_computation | async-start | bytes 2228224 | tf_op jit(solution)/shard_map/all_to_all | solution.py:338
  39.8 16.4 %all-to-all-done = bf16[16,8,4352]{2,1,0:T(8,128)(2,1)S(1)} async-done(((bf16[16,8,4352]{2,1,0:T(8,128)(2,1)}), bf16[16,8,4352]{2,1,0:T(8,128)(2,1)S(1)}, u32[]{:S(2)}, u32[]{:S(2)}) %all-to-all-start) | async-done | bytes 1114144 | tf_op jit(solution)/shard_map/all_to_all | solution.py:338
  56.2 2.5 %collective-permute-start.10 = (bf16[128,4352]{1,0:T(8,128)(2,1)S(1)}, bf16[128,4352]{1,0:T(8,128)(2,1)S(1)}, u32[]{:S(2)}, u32[]{:S(2)}) collective-permute-start(bf16[128,4352]{1,0:T(8,128)(2,1)S(1)} %bitcast.21), channel_id=1, source_target_pairs={{0,6},{1,7},{2,0},{3,1},{4,2},{5,3},{6,4},{7,5},{8,14},{9,15},{10,... | collective-permute-start | bytes 3342344 | tf_op jit(solution)/shard_map/ppermute | solution.py:288
  58.6 0.0 collective-permute-start.9
  58.6 1.1 constant_dynamic-slice_fusion.refs_0_
  59.7 2.7 %collective-permute-start.1 = (bf16[64,4096]{1,0:T(8,128)(2,1)S(1)}, bf16[64,4096]{1,0:T(8,128)(2,1)S(1)}, u32[]{:S(2)}, u32[]{:S(2)}) collective-permute-start(bf16[64,4096]{1,0:T(8,128)(2,1)S(1)} %constant_dynamic-slice_fusion.refs_0_), channel_id=1, source_target_pairs={{0,6},{1,7},{2,0},{3,1},{4,2},{5,3},{6,4},{7,5},{8,14},{9,15},{10,... | collective-permute-start | bytes 1572872 | tf_op jit(solution)/shard_map/ppermute | solution.py:288
  62.5 0.0 collective-permute-start
  62.5 28.2 %collective-permute-done.1.refs_2_ = bf16[64,4096]{1,0:T(8,128)(2,1)S(1)} collective-permute-done((bf16[64,4096]{1,0:T(8,128)(2,1)S(1)}, bf16[64,4096]{1,0:T(8,128)(2,1)S(1)}, u32[]{:S(2)}, u32[]{:S(2)}) %collective-permute-start.1) | collective-permute-done | bytes 524320 | tf_op jit(solution)/shard_map/ppermute | solution.py:288
  90.7 3.5 %collective-permute-start.3 = (bf16[32,4096]{1,0:T(8,128)(2,1)S(1)}, bf16[32,4096]{1,0:T(8,128)(2,1)S(1)}, u32[]{:S(2)}, u32[]{:S(2)}) collective-permute-start(bf16[32,4096]{1,0:T(8,128)(2,1)S(1)} %slice.37), channel_id=1, source_target_pairs={{0,6},{1,7},{2,0},{3,1},{4,2},{5,3},{6,4},{7,5},{8,14},{9,15},{10,... | collective-permute-start | bytes 786440 | tf_op jit(solution)/shard_map/ppermute | solution.py:288
  94.2 0.0 collective-permute-done.refs_1_
  94.2 0.0 copy-start.13
  94.2 0.1 collective-permute-start.2
  94.3 4.4 %collective-permute-start.4 = (bf16[64,4096]{1,0:T(8,128)(2,1)S(1)}, bf16[64,4096]{1,0:T(8,128)(2,1)S(1)}, u32[]{:S(2)}, u32[]{:S(2)}) collective-permute-start(bf16[64,4096]{1,0:T(8,128)(2,1)S(1)} %constant_dynamic-slice_fusion.refs_0_), channel_id=1, source_target_pairs={{0,1},{1,0},{2,3},{3,2},{4,5},{5,4},{6,7},{7,6},{8,9},{9,8},{10,11... | collective-permute-start | bytes 1572872 | tf_op jit(solution)/shard_map/ppermute | solution.py:292
  98.6 0.0 collective-permute-done.3.refs_4_
  98.6 3.7 %collective-permute-start.6 = (bf16[64,4096]{1,0:T(8,128)(2,1)S(1)}, bf16[64,4096]{1,0:T(8,128)(2,1)S(1)}, u32[]{:S(2)}, u32[]{:S(2)}) collective-permute-start(bf16[64,4096]{1,0:T(8,128)(2,1)S(1)} %collective-permute-done.1.refs_2_), channel_id=1, source_target_pairs={{0,1},{1,0},{2,3},{3,2},{4,5},{5,4},{6,7},{7,6},{8,9},{9,8},{10,11... | collective-permute-start | bytes 1572872 | tf_op jit(solution)/shard_map/ppermute | solution.py:292
  102.3 0.0 collective-permute-done.2.refs_3_
  102.3 3.8 %collective-permute-start.5 = (bf16[64,4096]{1,0:T(8,128)(2,1)S(1)}, bf16[64,4096]{1,0:T(8,128)(2,1)S(1)}, u32[]{:S(2)}, u32[]{:S(2)}) collective-permute-start(bf16[64,4096]{1,0:T(8,128)(2,1)S(1)} %collective-permute-done.refs_1_), channel_id=1, source_target_pairs={{0,1},{1,0},{2,3},{3,2},{4,5},{5,4},{6,7},{7,6},{8,9},{9,8},{10,11... | collective-permute-start | bytes 1572872 | tf_op jit(solution)/shard_map/ppermute | solution.py:292
  106.1 0.1 collective-permute-start.8
  106.2 0.4 collective-permute-start.7
  106.6 1.0 slice.39
  107.7 0.8 slice.38
  108.5 0.0 collective-permute-done.4.refs_5_
  108.5 0.1 collective-permute-start.12
  108.6 1.4 collective-permute-start.11
  110.1 0.0 collective-permute-done.6.refs_7_
  110.1 0.7 collective-permute-start.13
  110.8 0.1 collective-permute-start.15
  110.9 0.0 collective-permute-done.5.refs_6_
  110.9 0.5 collective-permute-start.14
  111.4 0.1 copy-done.12
  111.5 0.2 copy-done.8
  111.7 0.1 tile.21
  111.8 11.2 %collective-permute-done.12.refs_4_ = bf16[128,2176]{1,0:T(8,128)(2,1)} collective-permute-done((bf16[128,2176]{1,0:T(8,128)(2,1)}, bf16[128,2176]{1,0:T(8,128)(2,1)}, u32[]{:S(2)}, u32[]{:S(2)}) %collective-permute-start.12) | collective-permute-done | bytes 557088 | tf_op jit(solution)/shard_map/ppermute | solution.py:288
  123.0 0.9 collective-permute-start.17
  124.0 0.1 collective-permute-done.11.refs_3_
  124.1 1.2 collective-permute-start.16
  125.3 0.7 stack.35.base_ref
  126.0 0.6 broadcast_in_dim.180.noise_ref
  126.6 6.9 %score.1 = (f32[40,128]{1,0:T(8,128)}, f32[16,128]{1,0:T(8,128)}) custom-call(s32[8]{0:T(128)} %stack.35.base_ref, bf16[128,4352]{1,0:T(8,128)(2,1)} %bitcast.24, f32[8,128]{1,0:T(8,128)} %broadcast_in_dim.180.noise_ref, bf16[64,4096]{1,0:T(8,128)(2,1)} %copy-done.3, bf16[64,4096]{1,0:T(8,128)(2,1)} %copy-done.5, bf16[64,4096]{1,0:T(8,128)(2,1)} %copy-done.4, ...), custom_call_target="tpu_custom_call" | custom-call | flops 1000000000 | bytes 6000000 | tf_op jit(solution)/shard_map/score/pallas_call | solution.py:189
  133.4 0.7 broadcast_in_dim.181
  134.2 12.2 %all_to_all.15.parts_ref = f32[16,40,128]{2,1,0:T(8,128)} all-to-all(f32[16,40,128]{2,1,0:T(8,128)S(1)} %broadcast_in_dim.181), channel_id=1, replica_groups=mesh['tomo'=16,'cls'=8] {'tomo'}, dimensions={0} | all-to-all | bytes 655360 | tf_op jit(solution)/shard_map/all_to_all | solution.py:346
  146.4 1.8 %weights.1 = (f32[8,32]{1,0:T(8,128)}, bf16[8,64,128]{2,1,0:T(8,128)(2,1)}) custom-call(s32[1]{0:T(128)} %bitcast.at_ref, f32[16,40,128]{2,1,0:T(8,128)} %all_to_all.15.parts_ref, f32[16,128]{1,0:T(8,128)} %get-tuple-element.10.codes_ref), custom_call_target="tpu_custom_call" | custom-call | tf_op jit(solution)/shard_map/weights/pallas_call | solution.py:236
  148.2 11.0 %all_to_all.16.coef_ref = bf16[8,64,128]{2,1,0:T(8,128)(2,1)} all-to-all(bf16[8,64,128]{2,1,0:T(8,128)(2,1)} %get-tuple-element.12), channel_id=1, replica_groups=mesh['tomo'=16,'cls'=8] {'cls'}, dimensions={0} | all-to-all | bytes 262144 | tf_op jit(solution)/shard_map/all_to_all | solution.py:348
  159.2 0.0 collective-permute-done.16.refs_8_
  159.2 5.9 %sums.1 = (f32[64,4096]{1,0:T(8,128)}, f32[64,64]{1,0:T(8,128)}) custom-call(s32[8]{0:T(128)} %stack.35.base_ref, bf16[8,64,128]{2,1,0:T(8,128)(2,1)} %all_to_all.16.coef_ref, bf16[128,4352]{1,0:T(8,128)(2,1)} %bitcast.25, bf16[128,4352]{1,0:T(8,128)(2,1)} %copy-done.2, bf16[128,4352]{1,0:T(8,128)(2,1)} %copy-done.1, ...), custom_call_target="tpu_custom_call" | custom-call | tf_op jit(solution)/shard_map/sums/pallas_call | solution.py:274
  (40 shorter events, 0.1 us)
Async XLA Ops:
  31.2 25.0 %all-to-all-start = ((bf16[16,8,4352]{2,1,0:T(8,128)(2,1)}), bf16[16,8,4352]{2,1,0:T(8,128)(2,1)S(1)}, u32[]{:S(2)}, u32[]{:S(2)}) async-start(bf16[16,8,4352]{2,1,0:T(8,128)(2,1)} %dft.1), calls=%async_computation | async-start | bytes 2228224 | tf_op jit(solution)/shard_map/all_to_all | solution.py:338
  56.2 53.9 %copy-start = (bf16[16,8,4352]{2,1,0:T(8,128)(2,1)}, bf16[16,8,4352]{2,1,0:T(8,128)(2,1)S(1)}, u32[]{:S(2)}) copy-start(bf16[16,8,4352]{2,1,0:T(8,128)(2,1)S(1)} %all-to-all-done) | copy-start | bytes 3342340
  56.2 50.0 %collective-permute-start.10 = (bf16[128,4352]{1,0:T(8,128)(2,1)S(1)}, bf16[128,4352]{1,0:T(8,128)(2,1)S(1)}, u32[]{:S(2)}, u32[]{:S(2)}) collective-permute-start(bf16[128,4352]{1,0:T(8,128)(2,1)S(1)} %bitcast.21), channel_id=1, source_target_pairs={{0,6},{1,7},{2,0},{3,1},{4,2},{5,3},{6,4},{7,5},{8,14},{9,15},{10,... | collective-permute-start | bytes 3342344 | tf_op jit(solution)/shard_map/ppermute | solution.py:288
  58.6 47.6 %collective-permute-start.9 = (bf16[128,4352]{1,0:T(8,128)(2,1)S(1)}, bf16[128,4352]{1,0:T(8,128)(2,1)S(1)}, u32[]{:S(2)}, u32[]{:S(2)}) collective-permute-start(bf16[128,4352]{1,0:T(8,128)(2,1)S(1)} %bitcast.22), channel_id=1, source_target_pairs={{0,2},{1,3},{2,4},{3,5},{4,6},{5,7},{6,0},{7,1},{8,10},{9,11},{10,... | collective-permute-start | bytes 3342344 | tf_op jit(solution)/shard_map/ppermute | solution.py:288
  59.7 48.8 %copy-start.3 = (bf16[64,4096]{1,0:T(8,128)(2,1)}, bf16[64,4096]{1,0:T(8,128)(2,1)S(1)}, u32[]{:S(2)}) copy-start(bf16[64,4096]{1,0:T(8,128)(2,1)S(1)} %constant_dynamic-slice_fusion.refs_0_) | copy-start | bytes 1572868
  59.7 30.9 %collective-permute-start.1 = (bf16[64,4096]{1,0:T(8,128)(2,1)S(1)}, bf16[64,4096]{1,0:T(8,128)(2,1)S(1)}, u32[]{:S(2)}, u32[]{:S(2)}) collective-permute-start(bf16[64,4096]{1,0:T(8,128)(2,1)S(1)} %constant_dynamic-slice_fusion.refs_0_), channel_id=1, source_target_pairs={{0,6},{1,7},{2,0},{3,1},{4,2},{5,3},{6,4},{7,5},{8,14},{9,15},{10,... | collective-permute-start | bytes 1572872 | tf_op jit(solution)/shard_map/ppermute | solution.py:288
  62.5 31.7 %collective-permute-start = (bf16[64,4096]{1,0:T(8,128)(2,1)S(1)}, bf16[64,4096]{1,0:T(8,128)(2,1)S(1)}, u32[]{:S(2)}, u32[]{:S(2)}) collective-permute-start(bf16[64,4096]{1,0:T(8,128)(2,1)S(1)} %constant_dynamic-slice_fusion.refs_0_), channel_id=1, source_target_pairs={{0,2},{1,3},{2,4},{3,5},{4,6},{5,7},{6,0},{7,1},{8,10},{9,11},{10,... | collective-permute-start | bytes 1572872 | tf_op jit(solution)/shard_map/ppermute | solution.py:288
  90.6 20.2 %copy-start.4 = (bf16[64,4096]{1,0:T(8,128)(2,1)}, bf16[64,4096]{1,0:T(8,128)(2,1)S(1)}, u32[]{:S(2)}) copy-start(bf16[64,4096]{1,0:T(8,128)(2,1)S(1)} %collective-permute-done.1.refs_2_) | copy-start | bytes 1572868
  90.7 8.0 %collective-permute-start.3 = (bf16[32,4096]{1,0:T(8,128)(2,1)S(1)}, bf16[32,4096]{1,0:T(8,128)(2,1)S(1)}, u32[]{:S(2)}, u32[]{:S(2)}) collective-permute-start(bf16[32,4096]{1,0:T(8,128)(2,1)S(1)} %slice.37), channel_id=1, source_target_pairs={{0,6},{1,7},{2,0},{3,1},{4,2},{5,3},{6,4},{7,5},{8,14},{9,15},{10,... | collective-permute-start | bytes 786440 | tf_op jit(solution)/shard_map/ppermute | solution.py:288
  94.2 16.7 %copy-start.5 = (bf16[64,4096]{1,0:T(8,128)(2,1)}, bf16[64,4096]{1,0:T(8,128)(2,1)S(1)}, u32[]{:S(2)}) copy-start(bf16[64,4096]{1,0:T(8,128)(2,1)S(1)} %collective-permute-done.refs_1_) | copy-start | bytes 1572868
  94.2 17.5 %copy-start.13 = (f32[8]{0:T(128)S(1)}, f32[8]{0:T(128)}, u32[]{:S(2)}) copy-start(f32[8]{0:T(128)} %param.12) | copy-start | bytes 100
  94.2 8.1 %collective-permute-start.2 = (bf16[32,4096]{1,0:T(8,128)(2,1)S(1)}, bf16[32,4096]{1,0:T(8,128)(2,1)S(1)}, u32[]{:S(2)}, u32[]{:S(2)}) collective-permute-start(bf16[32,4096]{1,0:T(8,128)(2,1)S(1)} %slice.36), channel_id=1, source_target_pairs={{0,2},{1,3},{2,4},{3,5},{4,6},{5,7},{6,0},{7,1},{8,10},{9,11},{10,... | collective-permute-start | bytes 786440 | tf_op jit(solution)/shard_map/ppermute | solution.py:288
  94.3 14.3 %collective-permute-start.4 = (bf16[64,4096]{1,0:T(8,128)(2,1)S(1)}, bf16[64,4096]{1,0:T(8,128)(2,1)S(1)}, u32[]{:S(2)}, u32[]{:S(2)}) collective-permute-start(bf16[64,4096]{1,0:T(8,128)(2,1)S(1)} %constant_dynamic-slice_fusion.refs_0_), channel_id=1, source_target_pairs={{0,1},{1,0},{2,3},{3,2},{4,5},{5,4},{6,7},{7,6},{8,9},{9,8},{10,11... | collective-permute-start | bytes 1572872 | tf_op jit(solution)/shard_map/ppermute | solution.py:292
  98.6 12.8 %copy-start.9 = (bf16[32,4096]{1,0:T(8,128)(2,1)}, bf16[32,4096]{1,0:T(8,128)(2,1)S(1)}, u32[]{:S(2)}) copy-start(bf16[32,4096]{1,0:T(8,128)(2,1)S(1)} %collective-permute-done.3.refs_4_) | copy-start | bytes 786436
  98.6 11.4 %collective-permute-start.6 = (bf16[64,4096]{1,0:T(8,128)(2,1)S(1)}, bf16[64,4096]{1,0:T(8,128)(2,1)S(1)}, u32[]{:S(2)}, u32[]{:S(2)}) collective-permute-start(bf16[64,4096]{1,0:T(8,128)(2,1)S(1)} %collective-permute-done.1.refs_2_), channel_id=1, source_target_pairs={{0,1},{1,0},{2,3},{3,2},{4,5},{5,4},{6,7},{7,6},{8,9},{9,8},{10,11... | collective-permute-start | bytes 1572872 | tf_op jit(solution)/shard_map/ppermute | solution.py:292
  102.3 9.1 %copy-start.10 = (bf16[32,4096]{1,0:T(8,128)(2,1)}, bf16[32,4096]{1,0:T(8,128)(2,1)S(1)}, u32[]{:S(2)}) copy-start(bf16[32,4096]{1,0:T(8,128)(2,1)S(1)} %collective-permute-done.2.refs_3_) | copy-start | bytes 786436
  102.3 8.6 %collective-permute-start.5 = (bf16[64,4096]{1,0:T(8,128)(2,1)S(1)}, bf16[64,4096]{1,0:T(8,128)(2,1)S(1)}, u32[]{:S(2)}, u32[]{:S(2)}) collective-permute-start(bf16[64,4096]{1,0:T(8,128)(2,1)S(1)} %collective-permute-done.refs_1_), channel_id=1, source_target_pairs={{0,1},{1,0},{2,3},{3,2},{4,5},{5,4},{6,7},{7,6},{8,9},{9,8},{10,11... | collective-permute-start | bytes 1572872 | tf_op jit(solution)/shard_map/ppermute | solution.py:292
  106.1 5.6 %copy-start.1 = (bf16[128,4352]{1,0:T(8,128)(2,1)}, bf16[128,4352]{1,0:T(8,128)(2,1)S(1)}, u32[]{:S(2)}) copy-start(bf16[128,4352]{1,0:T(8,128)(2,1)S(1)} %collective-permute-done.10.refs_2_) | copy-start | bytes 3342340
  106.1 2.5 %collective-permute-start.8 = (bf16[32,4096]{1,0:T(8,128)(2,1)S(1)}, bf16[32,4096]{1,0:T(8,128)(2,1)S(1)}, u32[]{:S(2)}, u32[]{:S(2)}) collective-permute-start(bf16[32,4096]{1,0:T(8,128)(2,1)S(1)} %collective-permute-done.3.refs_4_), channel_id=1, source_target_pairs={{0,1},{1,0},{2,3},{3,2},{4,5},{5,4},{6,7},{7,6},{8,9},{9,8},{10,11... | collective-permute-start | bytes 786440 | tf_op jit(solution)/shard_map/ppermute | solution.py:292
  106.2 5.5 %copy-start.2 = (bf16[128,4352]{1,0:T(8,128)(2,1)}, bf16[128,4352]{1,0:T(8,128)(2,1)S(1)}, u32[]{:S(2)}) copy-start(bf16[128,4352]{1,0:T(8,128)(2,1)S(1)} %collective-permute-done.9.refs_1_) | copy-start | bytes 3342340
  106.2 4.6 %collective-permute-start.7 = (bf16[32,4096]{1,0:T(8,128)(2,1)S(1)}, bf16[32,4096]{1,0:T(8,128)(2,1)S(1)}, u32[]{:S(2)}, u32[]{:S(2)}) collective-permute-start(bf16[32,4096]{1,0:T(8,128)(2,1)S(1)} %collective-permute-done.2.refs_3_), channel_id=1, source_target_pairs={{0,1},{1,0},{2,3},{3,2},{4,5},{5,4},{6,7},{7,6},{8,9},{9,8},{10,11... | collective-permute-start | bytes 786440 | tf_op jit(solution)/shard_map/ppermute | solution.py:292
  108.5 2.9 %copy-start.6 = (bf16[64,4096]{1,0:T(8,128)(2,1)}, bf16[64,4096]{1,0:T(8,128)(2,1)S(1)}, u32[]{:S(2)}) copy-start(bf16[64,4096]{1,0:T(8,128)(2,1)S(1)} %collective-permute-done.4.refs_5_) | copy-start | bytes 1572868
  108.5 14.5 %collective-permute-start.12 = (bf16[128,2176]{1,0:T(8,128)(2,1)}, bf16[128,2176]{1,0:T(8,128)(2,1)}, u32[]{:S(2)}, u32[]{:S(2)}) collective-permute-start(bf16[128,2176]{1,0:T(8,128)(2,1)} %slice.39), channel_id=1, source_target_pairs={{0,6},{1,7},{2,0},{3,1},{4,2},{5,3},{6,4},{7,5},{8,14},{9,15},{10,... | collective-permute-start | bytes 1671176 | tf_op jit(solution)/shard_map/ppermute | solution.py:288
  108.6 2.8 %copy-start.11 = (bf16[32,4096]{1,0:T(8,128)(2,1)}, bf16[32,4096]{1,0:T(8,128)(2,1)S(1)}, u32[]{:S(2)}) copy-start(bf16[32,4096]{1,0:T(8,128)(2,1)S(1)} %collective-permute-done.8.refs_9_) | copy-start | bytes 786436
  108.6 15.5 %collective-permute-start.11 = (bf16[128,2176]{1,0:T(8,128)(2,1)}, bf16[128,2176]{1,0:T(8,128)(2,1)}, u32[]{:S(2)}, u32[]{:S(2)}) collective-permute-start(bf16[128,2176]{1,0:T(8,128)(2,1)} %slice.38), channel_id=1, source_target_pairs={{0,2},{1,3},{2,4},{3,5},{4,6},{5,7},{6,0},{7,1},{8,10},{9,11},{10,... | collective-permute-start | bytes 1671176 | tf_op jit(solution)/shard_map/ppermute | solution.py:288
  110.1 1.3 copy-start.7
  110.1 49.1 %collective-permute-start.13 = (bf16[128,4352]{1,0:T(8,128)(2,1)S(1)}, bf16[128,4352]{1,0:T(8,128)(2,1)}, u32[]{:S(2)}, u32[]{:S(2)}) collective-permute-start(bf16[128,4352]{1,0:T(8,128)(2,1)S(1)} %bitcast.23), channel_id=1, source_target_pairs={{0,1},{1,0},{2,3},{3,2},{4,5},{5,4},{6,7},{7,6},{8,9},{9,8},{10,11... | collective-permute-start | bytes 3342344 | tf_op jit(solution)/shard_map/ppermute | solution.py:292
  110.8 0.7 copy-start.12
  110.8 48.4 %collective-permute-start.15 = (bf16[128,4352]{1,0:T(8,128)(2,1)S(1)}, bf16[128,4352]{1,0:T(8,128)(2,1)}, u32[]{:S(2)}, u32[]{:S(2)}) collective-permute-start(bf16[128,4352]{1,0:T(8,128)(2,1)S(1)} %collective-permute-done.10.refs_2_), channel_id=1, source_target_pairs={{0,1},{1,0},{2,3},{3,2},{4,5},{5,4},{6,7},{7,6},{8,9},{9,8},{10,11... | collective-permute-start | bytes 3342344 | tf_op jit(solution)/shard_map/ppermute | solution.py:292
  110.9 0.8 copy-start.8
  110.9 48.3 %collective-permute-start.14 = (bf16[128,4352]{1,0:T(8,128)(2,1)S(1)}, bf16[128,4352]{1,0:T(8,128)(2,1)}, u32[]{:S(2)}, u32[]{:S(2)}) collective-permute-start(bf16[128,4352]{1,0:T(8,128)(2,1)S(1)} %collective-permute-done.9.refs_1_), channel_id=1, source_target_pairs={{0,1},{1,0},{2,3},{3,2},{4,5},{5,4},{6,7},{7,6},{8,9},{9,8},{10,11... | collective-permute-start | bytes 3342344 | tf_op jit(solution)/shard_map/ppermute | solution.py:292
  123.0 36.2 %collective-permute-start.17 = (bf16[128,2176]{1,0:T(8,128)(2,1)}, bf16[128,2176]{1,0:T(8,128)(2,1)}, u32[]{:S(2)}, u32[]{:S(2)}) collective-permute-start(bf16[128,2176]{1,0:T(8,128)(2,1)} %collective-permute-done.12.refs_4_), channel_id=1, source_target_pairs={{0,1},{1,0},{2,3},{3,2},{4,5},{5,4},{6,7},{7,6},{8,9},{9,8},{10,11... | collective-permute-start | bytes 1671176 | tf_op jit(solution)/shard_map/ppermute | solution.py:292
  124.1 35.1 %collective-permute-start.16 = (bf16[128,2176]{1,0:T(8,128)(2,1)}, bf16[128,2176]{1,0:T(8,128)(2,1)}, u32[]{:S(2)}, u32[]{:S(2)}) collective-permute-start(bf16[128,2176]{1,0:T(8,128)(2,1)} %collective-permute-done.11.refs_3_), channel_id=1, source_target_pairs={{0,1},{1,0},{2,3},{3,2},{4,5},{5,4},{6,7},{7,6},{8,9},{9,8},{10,11... | collective-permute-start | bytes 1671176 | tf_op jit(solution)/shard_map/ppermute | solution.py:292

commit v2 on v1

v2 whole, which is shorter than its diff:
```python
import math

import jax
import jax.numpy as jnp
import numpy as np
from jax import lax
from jax.experimental import pallas as pl
from jax.experimental.pallas import tpu as pltpu
from jax.sharding import PartitionSpec as P


VOX = 64
KB = 32
NSET = 16
ROT = 8
CAND = 4
PART = 8
ROWS = 16
COLS = 8
CLS_DEV = 4
CLS_ROWS = CLS_DEV * NSET
SLICE = 2 * KB**3 // ROWS
HALF = SLICE // 2
WIDTH = HALF + 128
CODE_AT = 64
CHUNK = 1024


def split_table(table):
    high = table.astype(jnp.bfloat16)
    low = (table - np.asarray(high, np.float32)).astype(jnp.bfloat16)
    return high, low


def dft_constants(half):
    frequency = np.arange(KB) - KB // 2
    residue = (frequency[:, None] * np.arange(VOX)[None, :]) % VOX
    radians = residue * (2.0 * math.pi / VOX)
    both = (np.stack([np.cos(radians), -np.sin(radians)]) / math.sqrt(VOX)).astype(np.float32)
    depth_table = np.kron(np.eye(4, dtype=np.float32), both.reshape(2 * KB, VOX))
    wz = np.concatenate(split_table(depth_table), axis=0)
    kept = both.reshape(2, 8, 2, 2, VOX)[:, :, half].reshape(2, KB // 2, VOX)
    wide = np.einsum("akx,pq->pxakq", kept, np.eye(PART, dtype=np.float32))
    wxh, wxl = split_table(wide.reshape(PART * VOX, KB * PART))
    high, low = split_table(both.reshape(2 * KB, VOX))
    wy = np.concatenate([high, high, low], axis=1)
    return wz, wxh, wxl, wy


def mask_rows(tomo_ref, wedge_ref, cand_ref, rot_ref, index):
    table = wedge_ref[...].reshape(4 * KB, KB).astype(jnp.float32).astype(jnp.bfloat16)
    source = lax.broadcasted_iota(jnp.int32, (KB, 128), 0)
    lane = lax.broadcasted_iota(jnp.int32, (KB, 128), 1)
    wide = jnp.dot(
        table, ((lane & 31) == source).astype(jnp.bfloat16), preferred_element_type=jnp.float32
    ).astype(jnp.bfloat16)
    index[...] = jnp.zeros_like(index)
    index[:1, :PART] = tomo_ref[...].astype(jnp.float32)
    index[CODE_AT : CODE_AT + CAND, :PART] = cand_ref[...].astype(jnp.float32)
    turned = index[...].T[:PART]
    index[:PART, :] = turned
    index[:PART, CODE_AT + 8 : CODE_AT + 8 + ROT] = rot_ref[...].astype(jnp.float32)
    local = jnp.broadcast_to(turned[:, :1].astype(jnp.int32) & 3, (PART, 128))
    local = jnp.concatenate([local] * KB, axis=0)
    row = lax.broadcasted_iota(jnp.int32, (KB * PART, 128), 0)
    col = lax.broadcasted_iota(jnp.int32, (KB * PART, 128), 1)
    pick = (((col & 31) == (row >> 3)) & ((col >> 5) == local)).astype(jnp.bfloat16)
    return jnp.dot(pick, wide, preferred_element_type=jnp.float32)


def dft_kernel(
    half,
    p_ref,
    wz_ref,
    wxh_ref,
    wxl_ref,
    wy_ref,
    tomo_ref,
    wedge_ref,
    cand_ref,
    rot_ref,
    out_ref,
    mid,
    last,
    masks,
    index,
):
    step = pl.program_id(0)
    for block in range(CHUNK // 256):
        data = p_ref[:, :, block * 256 : (block + 1) * 256].reshape(PART * VOX, 256)
        first = lax.dot_general(
            wz_ref[...], data, (((1,), (1,)), ((), ())), preferred_element_type=jnp.float32
        )
        first = first[: 8 * KB] + first[8 * KB :]
        high = first.astype(jnp.bfloat16)
        low = (first - high.astype(jnp.float32)).astype(jnp.bfloat16)
        second = (
            jnp.dot(high, wxh_ref[...], preferred_element_type=jnp.float32)
            + jnp.dot(low, wxh_ref[...], preferred_element_type=jnp.float32)
            + jnp.dot(high, wxl_ref[...], preferred_element_type=jnp.float32)
        )
        for yy in range(4):
            cos_rows = second[yy * 64 : yy * 64 + 32]
            sin_rows = second[yy * 64 + 32 : yy * 64 + 64]
            at = (step * (CHUNK // 64) + block * 4 + yy) * KB
            rows = pl.ds(pl.multiple_of(at, KB), KB)
            mid[0, rows, :] = cos_rows[:, :128] - sin_rows[:, 128:]
            mid[1, rows, :] = sin_rows[:, :128] + cos_rows[:, 128:]

    @pl.when(step == pl.num_programs(0) - 1)
    def _():
        masks[...] = mask_rows(tomo_ref, wedge_ref, cand_ref, rot_ref, index)
        for kz in range(KB):
            values = jnp.concatenate(
                [mid[part, pl.ds(kz, VOX, stride=KB), :] for part in range(2)], axis=1
            )
            top = values.astype(jnp.bfloat16)
            rest = (values - top.astype(jnp.float32)).astype(jnp.bfloat16)
            third = jnp.dot(
                wy_ref[...],
                jnp.concatenate([top, rest, top], axis=0),
                preferred_element_type=jnp.float32,
            )
            rows = pl.ds(kz, KB, stride=KB)
            last[0, rows, :] = third[:KB, :128] - third[KB:, 128:]
            last[1, rows, :] = third[KB:, :128] + third[:KB, 128:]
        for part in range(2):
            turned = last[part].T
            for k in range(16):
                kx = (k // 2) * 4 + half * 2 + k % 2
                keep = jnp.concatenate([masks[kx * PART : (kx + 1) * PART, :]] * 8, axis=1)
                piece = turned[k * PART : (k + 1) * PART, :] * keep
                at = (k % 2) * 1024
                out_ref[part * 8 + k // 2, :, at : at + 1024] = piece.astype(jnp.bfloat16)
        lane = lax.broadcasted_iota(jnp.int32, (PART, 128), 1)
        table = lambda kx: masks[kx * PART : (kx + 1) * PART, :]
        if half == 0:
            for group in range(8):
                plane = jnp.zeros((PART, 128), jnp.float32)
                for k in range(4):
                    plane = jnp.where((lane >> 5) == k, table(group * 4 + k), plane)
                plane = plane.astype(jnp.bfloat16)
                out_ref[group, :, HALF:] = plane
                out_ref[group + 8, :, HALF:] = plane
        else:
            codes = index[:PART, :]
            for target in range(ROWS):
                entry = jnp.where(lane < KB, table(target * 2), table(target * 2 + 1))
                entry = jnp.where(lane < 2 * KB, entry, codes)
                out_ref[target, :, HALF:] = entry.astype(jnp.bfloat16)


def spectra_call(half, particles, tomogram, wedge, candidates, rotations):
    tables = dft_constants(half)
    small = (tomogram, wedge, candidates, rotations)
    whole = lambda array: pl.BlockSpec(array.shape, lambda i, n=array.ndim: (0,) * n)
    return pl.pallas_call(
        lambda *refs: dft_kernel(half, *refs),
        grid=(VOX * VOX // CHUNK,),
        in_specs=[pl.BlockSpec((PART, VOX, CHUNK), lambda i: (0, 0, i))]
        + [whole(array) for array in tables + small],
        out_specs=pl.BlockSpec((ROWS, PART, WIDTH), lambda i: (0, 0, 0)),
        out_shape=jax.ShapeDtypeStruct((ROWS, PART, WIDTH), jnp.bfloat16),
        scratch_shapes=[
            pltpu.VMEM((2, VOX * KB, 128), jnp.float32),
            pltpu.VMEM((2, KB * KB, 128), jnp.float32),
            pltpu.VMEM((KB * PART, 128), jnp.float32),
            pltpu.VMEM((128, 128), jnp.float32),
        ],
        compiler_params=pltpu.CompilerParams(dimension_semantics=("arbitrary",)),
        cost_estimate=pl.CostEstimate(
            flops=10_000_000_000, bytes_accessed=6_000_000, transcendentals=0
        ),
    )(particles, *(jnp.asarray(table) for table in tables), *small)


CONTRACT = (((1,), (1,)), ((), ()))


def cls_of(col, index):
    x = ((col >> 1) + (0, 3, 1, 2)[index % 4]) & 3
    return (x << 1) + ((col & 1) ^ (index // 4))


def stacked_pieces(refs):
    return jnp.concatenate([ref[...] for ref in refs], axis=0)


def score_first_kernel(slots_ref, plane_ref, *refs):
    pieces, out_ref = refs[:-1], refs[-1]
    step = pl.program_id(0)
    values = stacked_pieces(pieces)
    row = lax.broadcasted_iota(jnp.int32, (128, 128), 0)
    col = lax.broadcasted_iota(jnp.int32, (128, 128), 1)
    term = None
    for k in range(2):
        spread = ((row >> 5) == 2 * step + k) & ((row & 31) == (col & 31))
        keep = jnp.dot(
            plane_ref[...], spread.astype(jnp.bfloat16), preferred_element_type=jnp.float32
        ).astype(jnp.bfloat16)
        power = jnp.zeros((COLS * CLS_ROWS, 128), jnp.float32)
        for j in range(8):
            at = k * 1024 + j * 128
            value = values[:, at : at + 128].astype(jnp.float32)
            power = power + value * value
        one = power.astype(jnp.bfloat16)
        left = power - one.astype(jnp.float32)
        two = left.astype(jnp.bfloat16)
        three = (left - two.astype(jnp.float32)).astype(jnp.bfloat16)
        for part in (three, two, one):
            more = lax.dot_general(part, keep, CONTRACT, preferred_element_type=jnp.float32)
            term = more if term is None else term + more

    @pl.when(step == 0)
    def _():
        out_ref[...] = -0.5 * term + lax.dot_general(
            values, slots_ref[...], CONTRACT, preferred_element_type=jnp.float32
        )

    @pl.when(step == 1)
    def _():
        out_ref[...] += -0.5 * term


def score_first_call(slots, pieces):
    return pl.pallas_call(
        score_first_kernel,
        grid=(2,),
        in_specs=[
            pl.BlockSpec((128, HALF), lambda i: (0, 0)),
            pl.BlockSpec((128, 128), lambda i: (0, HALF // 128)),
        ]
        + [pl.BlockSpec((CLS_ROWS, HALF), lambda i: (0, i))] * COLS,
        out_specs=pl.BlockSpec((COLS * CLS_ROWS, 128), lambda i: (0, 0)),
        out_shape=jax.ShapeDtypeStruct((COLS * CLS_ROWS, 128), jnp.float32),
        compiler_params=pltpu.CompilerParams(dimension_semantics=("arbitrary",)),
        cost_estimate=pl.CostEstimate(
            flops=1_000_000_000, bytes_accessed=5_000_000, transcendentals=0
        ),
        name="score0",
    )(slots, slots, *pieces)


def score_second_kernel(col_ref, slots_ref, code_ref, noise_ref, begun_ref, *refs):
    pieces, out_ref, codes_ref, table = refs[:COLS], refs[-3], refs[-2], refs[-1]
    step = pl.program_id(0)
    inner = lax.dot_general(
        stacked_pieces(pieces), slots_ref[...], CONTRACT, preferred_element_type=jnp.float32
    )

    @pl.when(step == 0)
    def _():
        table[...] = begun_ref[...] + inner

    @pl.when(step == 1)
    def _():
        table[...] += inner
        codes = code_ref[...].astype(jnp.float32).T[CODE_AT : CODE_AT + 16]
        codes_ref[...] = codes
        chosen = [jnp.zeros((NSET, 128), jnp.float32) for _ in range(CAND)]
        for index in range(COLS):
            first = cls_of(col_ref[0], index) * CLS_DEV
            for local in range(CLS_DEV):
                label = (first + local).astype(jnp.float32)
                at = index * CLS_ROWS + local * NSET
                block = table[at : at + NSET]
                for j in range(CAND):
                    chosen[j] = chosen[j] + jnp.where(codes[j : j + 1] == label, block, 0.0)
        copies = lax.broadcasted_iota(jnp.int32, (NSET, 128), 0).astype(jnp.float32)
        for r in range(ROT):
            hit = codes[8 + r : 9 + r] == copies
            for j in range(CAND):
                value = jnp.sum(jnp.where(hit, chosen[j], 0.0), axis=0, keepdims=True)
                out_ref[0, j * ROT + r : j * ROT + r + 1, :] = value
        out_ref[0, CAND * ROT :, :] = jnp.zeros((8, 128), jnp.float32)
        out_ref[0, CAND * ROT : CAND * ROT + 1, :PART] = noise_ref[...]
        whole = out_ref[0]
        for target in range(1, ROWS):
            out_ref[target] = whole


def score_second_call(col, slots, noise, begun, pieces):
    return pl.pallas_call(
        score_second_kernel,
        grid=(2,),
        in_specs=[
            pl.BlockSpec(memory_space=pltpu.SMEM),
            pl.BlockSpec((128, 1024), lambda i: (0, i)),
            pl.BlockSpec((128, 128), lambda i: (0, HALF // 128)),
            pl.BlockSpec((1, PART), lambda i: (0, 0)),
            pl.BlockSpec((COLS * CLS_ROWS, 128), lambda i: (0, 0)),
        ]
        + [pl.BlockSpec((CLS_ROWS, 1024), lambda i: (0, 2 + i))] * COLS,
        out_specs=(
            pl.BlockSpec((ROWS, CAND * ROT + 8, 128), lambda i: (0, 0, 0)),
            pl.BlockSpec((16, 128), lambda i: (0, 0)),
        ),
        out_shape=(
            jax.ShapeDtypeStruct((ROWS, CAND * ROT + 8, 128), jnp.float32),
            jax.ShapeDtypeStruct((16, 128), jnp.float32),
        ),
        scratch_shapes=[pltpu.VMEM((COLS * CLS_ROWS, 128), jnp.float32)],
        compiler_params=pltpu.CompilerParams(dimension_semantics=("arbitrary",)),
        cost_estimate=pl.CostEstimate(
            flops=1_000_000_000, bytes_accessed=4_000_000, transcendentals=0
        ),
        name="score1",
    )(col, slots, slots, noise, begun, *pieces)


def softmax_kernel(at_ref, parts_ref, codes_ref, post_ref, coef_ref, turned):
    total = parts_ref[0, : CAND * ROT]
    noise = parts_ref[0, CAND * ROT :]
    for row in range(1, ROWS):
        total = total + parts_ref[row, : CAND * ROT]
        noise = noise + pltpu.roll(parts_ref[row, CAND * ROT :], row * PART, 1)
    logits = noise[:1] * total
    peak = jnp.max(logits, axis=0, keepdims=True)
    weight = jnp.exp(logits - peak)
    posterior = weight / jnp.sum(weight, axis=0, keepdims=True)
    padded = jnp.concatenate([posterior, jnp.zeros((96, 128), jnp.float32)], axis=0)
    turned[...] = padded.T
    own = turned[pl.ds(pl.multiple_of(at_ref[0] * PART, PART), PART), :]
    post_ref[...] = own[:, : CAND * ROT]
    rounded = posterior.astype(jnp.bfloat16).astype(jnp.float32)
    codes = codes_ref[...]
    copies = lax.broadcasted_iota(jnp.int32, (NSET, 128), 0).astype(jnp.float32)
    spread = []
    for j in range(CAND):
        value = jnp.zeros((NSET, 128), jnp.float32)
        for r in range(ROT):
            hit = codes[8 + r : 9 + r] == copies
            value = value + jnp.where(hit, rounded[j * ROT + r : j * ROT + r + 1], 0.0)
        spread.append(value)
    for label in range(COLS * CLS_DEV):
        value = jnp.zeros((NSET, 128), jnp.float32)
        for j in range(CAND):
            value = value + jnp.where(codes[j : j + 1] == float(label), spread[j], 0.0)
        at = (label % CLS_DEV) * NSET
        coef_ref[label // CLS_DEV, at : at + NSET, :] = value.astype(jnp.bfloat16)


def softmax_call(row_index, parts, codes):
    vmem = pl.BlockSpec(memory_space=pltpu.VMEM)
    return pl.pallas_call(
        softmax_kernel,
        in_specs=[pl.BlockSpec(memory_space=pltpu.SMEM), vmem, vmem],
        out_specs=(vmem, vmem),
        out_shape=(
            jax.ShapeDtypeStruct((PART, CAND * ROT), jnp.float32),
            jax.ShapeDtypeStruct((COLS, CLS_DEV * NSET, 128), jnp.bfloat16),
        ),
        scratch_shapes=[pltpu.VMEM((128, 128), jnp.float32)],
        name="weights",
    )(row_index, parts, codes)


def sums_kernel(half, col_ref, coef_ref, *refs):
    pieces = refs[:COLS]
    coefs = [coef_ref[cls_of(col_ref[0], slot)] for slot in range(COLS)]

    def combine(blocks):
        total = None
        for coef, ref in zip(coefs, blocks):
            term = jnp.dot(coef, ref[...], preferred_element_type=jnp.float32)
            total = term if total is None else total + term
        return total

    if half == 0:
        refs[COLS][...] = combine(pieces)
        return
    class_ref, wedge_ref = refs[-2], refs[-1]
    class_ref[...] = combine(pieces)

    @pl.when(pl.program_id(0) == 0)
    def _():
        wedge_ref[...] = combine(refs[COLS : 2 * COLS])[:, :64]


def sums_call(half, col, coefs, pieces, begun=None):
    block = HALF // 2
    spec = pl.BlockSpec((128, block), lambda i: (0, i))
    in_specs = [
        pl.BlockSpec(memory_space=pltpu.SMEM),
        pl.BlockSpec((COLS, CLS_ROWS, 128), lambda i: (0, 0, 0)),
    ] + [spec] * COLS
    operands = [col, coefs] + list(pieces)
    out_specs = [pl.BlockSpec((CLS_ROWS, block), lambda i: (0, 2 * half + i))]
    out_shape = [jax.ShapeDtypeStruct((CLS_ROWS, SLICE), jnp.float32)]
    aliases = {}
    if half == 1:
        in_specs += [pl.BlockSpec((128, 128), lambda i: (0, HALF // 128))] * COLS
        operands += list(pieces)
        aliases = {len(operands): 0}
        in_specs.append(pl.BlockSpec(memory_space=pl.ANY))
        operands.append(begun)
        out_specs.append(pl.BlockSpec((CLS_ROWS, 64), lambda i: (0, 0)))
        out_shape.append(jax.ShapeDtypeStruct((CLS_ROWS, 64), jnp.float32))
    return pl.pallas_call(
        lambda *refs: sums_kernel(half, *refs),
        grid=(2,),
        in_specs=in_specs,
        out_specs=out_specs,
        out_shape=out_shape,
        input_output_aliases=aliases,
        compiler_params=pltpu.CompilerParams(dimension_semantics=("arbitrary",)),
        cost_estimate=pl.CostEstimate(
            flops=300_000_000, bytes_accessed=5_000_000, transcendentals=0
        ),
    )(*operands)


def along_x(value, hops):
    pairs = [(i, ((i // 2 + hops) % 4) * 2 + i % 2) for i in range(COLS)]
    return lax.ppermute(value, "cls", pairs)


def other_core(value):
    return lax.ppermute(value, "cls", [(i, i ^ 1) for i in range(COLS)])


def around(value, forward):
    ahead = along_x(value, 1)
    behind = along_x(value, -1)
    other = other_core(value)
    far = along_x(ahead, 1) if forward else along_x(behind, -1)
    other_near = [other_core(ahead), other_core(behind)]
    other_far = other_core(far)
    return [value, ahead, behind, far, other] + other_near + [other_far]


def inner(particles, inverse_noise, tomogram, candidates, rotations, wedge, references):
    row = lax.axis_index("tomo")
    col = lax.axis_index("cls")
    row_ref = row.astype(jnp.int32)[None]
    col_ref = col.astype(jnp.int32)[None]

    flat_refs = references.reshape(CLS_ROWS, 2 * KB**3)
    ref_slice = lax.dynamic_slice(flat_refs, (0, row * SLICE), (CLS_ROWS, SLICE))
    ref_pieces = around(ref_slice, True)

    small = (tomogram[None], wedge, candidates.T, rotations)
    slots, slot_pieces = [], []
    for half in (0, 1):
        spectra = spectra_call(half, particles, *small)
        moved = lax.all_to_all(spectra, "tomo", 0, 0, tiled=True)
        slots.append(moved.reshape(ROWS * PART, WIDTH))
        slot_pieces.append(around(slots[half], half == 0))

    begun = score_first_call(slots[0], ref_pieces)
    copies, codes = score_second_call(
        col_ref, slots[1], inverse_noise[None], begun, ref_pieces
    )
    parts = lax.all_to_all(copies, "tomo", 0, 0, tiled=True)
    posterior, coefs = softmax_call(row_ref, parts, codes)
    coefs = lax.all_to_all(coefs, "cls", 0, 0, tiled=True)
    (class_sums,) = sums_call(0, col_ref, coefs, slot_pieces[0])
    class_sums, wedge_sums = sums_call(1, col_ref, coefs, slot_pieces[1], class_sums)
    return (
        posterior,
        class_sums.reshape(CLS_DEV, NSET, SLICE),
        wedge_sums.reshape(CLS_DEV, NSET, 64),
    )


def solution(mesh):
    return jax.shard_map(
        inner,
        mesh=mesh,
        in_specs=(
            P(("tomo", "cls"), None, None),
            P(("tomo", "cls")),
            P(("tomo", "cls")),
            P(("tomo", "cls"), None),
            P(("tomo", "cls"), None),
            P("tomo", None, None),
            P("cls", None, None),
        ),
        out_specs=(P(("tomo", "cls"), None), P("cls", None, "tomo"), P("cls", None, "tomo")),
        check_vma=False,
    )
```

time: 166 us -> 134 us (0.81)
  waiting for transfers between devices: 55.9 us -> 23.6 us
  local copies, waits for them, and re-layouts: 8.61 us -> 1.91 us
  starting transfers between devices: 34.6 us -> 39.4 us
  blocking collectives: 23.2 us -> 27.6 us
  other arithmetic: 2.41 us -> 0 us
    ppermute x8 -> x9, waiting for transfers between devices: 39.6 us -> 15.1 us  [along_x(): return lax.ppermute(value, 'cls', pairs)]
    all_to_all x1 -> x2, waiting for transfers between devices: 16.4 us -> 6.54 us  [inner(): moved = lax.all_to_all(spectra, 'tomo', 0, 0, tiled=True)]
    all_to_all x1 -> x2, starting transfers between devices: 8.59 us -> 14.8 us  [inner(): moved = lax.all_to_all(spectra, 'tomo', 0, 0, tiled=True)]
    all_to_all x1, blocking collectives: 12.2 us -> 15.3 us  [inner(): parts = lax.all_to_all(copies, 'tomo', 0, 0, tiled=True)]
    ppermute x10 -> x12, starting transfers between devices: 15.7 us -> 12.8 us  [other_core(): return lax.ppermute(value, 'cls', [(i, i ^ 1) for i in range(COLS)])]
    slice x5 -> x0, local copies, waits for them, and re-layouts: 2.69 us -> none  [the longest x2 1.87 us: inner(): slot_pieces = around(slots, lambda v: v[:, :HALF], lambda v: v[:, HALF:])]
    broadcast_in_dim x11 -> x0, local copies, waits for them, and re-layouts: 1.91 us -> none  [the longest x1 0.75 us: inner(): copies = jnp.broadcast_to(partial[None], (ROWS,) + partial.shape)]
    ppermute x10 -> x12, waiting for transfers between devices: 0.03 us -> 1.91 us  [other_core(): return lax.ppermute(value, 'cls', [(i, i ^ 1) for i in range(COLS)])]
  transfers between devices with their start and end apart: 19 -> 23, of which waited for: 4 -> 5; matrix products, arithmetic and copies ran while one was open for 3% -> 0% of each run, Pallas kernels for 5% -> 27%
where the time goes in v2:
time: 134 us
  Pallas kernels  40.2 us (30%)
  starting transfers between devices  39.4 us (29%)
  blocking collectives  27.6 us (21%)
  waiting for transfers between devices  23.6 us (18%)
  local copies, waits for them, and re-layouts  1.91 us (1%)
    pallas_call x2, Pallas kernels, spectra_call(): pl.pallas_call(lambda *refs: dft_kernel(half, *refs), grid=(VOX * VOX //...  22.6 us
    all_to_all x1, blocking collectives, inner(): parts = lax.all_to_all(copies, 'tomo', 0, 0, tiled=True)  15.3 us
    ppermute x9, waiting for transfers between devices, along_x(): return lax.ppermute(value, 'cls', pairs)  15.1 us
    all_to_all x2, starting transfers between devices, inner(): moved = lax.all_to_all(spectra, 'tomo', 0, 0, tiled=True)  14.8 us
    ppermute x12, starting transfers between devices, other_core(): return lax.ppermute(value, 'cls', [(i, i ^ 1) for i in range(COLS)])  12.8 us
    all_to_all x1, blocking collectives, inner(): coefs = lax.all_to_all(coefs, 'cls', 0, 0, tiled=True)  12.3 us
    ppermute x9, starting transfers between devices, along_x(): return lax.ppermute(value, 'cls', pairs)  11.8 us
    pallas_call x2, Pallas kernels, sums_call(): pl.pallas_call(lambda *refs: sums_kernel(half, *refs), grid=(2,), in_spec...  6.88 us
  transfers between devices with their start and end apart: 23, of which 5 were waited for; matrix products, arithmetic and copies ran while one was open for 0% of the time, Pallas kernels for 27%

profile of v2, /device:TPU:1, one launch (start us, length us, event | category | flops | bytes accessed | tf_op | source)
XLA Modules:
  0.0 133.6 jit_solution(15203258308301871738)
XLA Ops:
  0.6 1.1 constant_dynamic-slice_fusion.refs_0_
  1.7 0.0 copy-start.2
  1.7 2.1 %collective-permute-start = (bf16[64,4096]{1,0:T(8,128)(2,1)S(1)}, bf16[64,4096]{1,0:T(8,128)(2,1)S(1)}, u32[]{:S(2)}, u32[]{:S(2)}) collective-permute-start(bf16[64,4096]{1,0:T(8,128)(2,1)S(1)} %constant_dynamic-slice_fusion.refs_0_), channel_id=1, source_target_pairs={{0,2},{1,3},{2,4},{3,5},{4,6},{5,7},{6,0},{7,1},{8,10},{9,11},{10,... | collective-permute-start | bytes 1572872 | tf_op jit(solution)/shard_map/ppermute | solution.py:415
  3.8 1.3 %collective-permute-start.1 = (bf16[64,4096]{1,0:T(8,128)(2,1)S(1)}, bf16[64,4096]{1,0:T(8,128)(2,1)S(1)}, u32[]{:S(2)}, u32[]{:S(2)}) collective-permute-start(bf16[64,4096]{1,0:T(8,128)(2,1)S(1)} %constant_dynamic-slice_fusion.refs_0_), channel_id=1, source_target_pairs={{0,6},{1,7},{2,0},{3,1},{4,2},{5,3},{6,4},{7,5},{8,14},{9,15},{10,... | collective-permute-start | bytes 1572872 | tf_op jit(solution)/shard_map/ppermute | solution.py:415
  5.2 1.2 collective-permute-start.3
  6.4 11.3 %shard_map.167 = bf16[16,8,2176]{2,1,0:T(8,128)(2,1)} custom-call(bf16[8,64,4096]{2,1,0:T(8,128)(2,1)} %refs_0_.3, bf16[512,256]{1,0:T(8,128)(2,1)} %constant.27.clone.refs_1_, bf16[512,256]{1,0:T(8,128)(2,1)} %constant.28.clone.refs_2_, bf16[512,256]{1,0:T(8,128)(2,1)} %constant.29.clone.refs_3_, bf16[64,192]{1,0:T(8,128)(2,1)} %constant.30.clone.refs_4_, ...), custom_call_target="tpu_custom_call" | custom-call | flops 10000000000 | bytes 6000000 | tf_op jit(solution)/shard_map/pallas_call | solution.py:157
  17.7 0.0 copy-done.2
  17.7 7.9 %all-to-all-start.1 = ((bf16[16,8,2176]{2,1,0:T(8,128)(2,1)}), bf16[16,8,2176]{2,1,0:T(8,128)(2,1)S(1)}, u32[]{:S(2)}, u32[]{:S(2)}) async-start(bf16[16,8,2176]{2,1,0:T(8,128)(2,1)} %shard_map.167), calls=%async_computation.1 | async-start | bytes 1114112 | tf_op jit(solution)/shard_map/all_to_all | solution.py:446
  25.6 0.0 collective-permute-done.refs_1_
  25.6 0.0 copy-start.7
  25.6 0.1 collective-permute-start.2
  25.7 0.6 collective-permute-start.4
  26.2 11.3 %shard_map.166 = bf16[16,8,2176]{2,1,0:T(8,128)(2,1)} custom-call(bf16[8,64,4096]{2,1,0:T(8,128)(2,1)} %refs_0_.3, bf16[512,256]{1,0:T(8,128)(2,1)} %constant.27.clone.refs_1_, bf16[512,256]{1,0:T(8,128)(2,1)} %constant.31.clone.refs_2_, bf16[512,256]{1,0:T(8,128)(2,1)} %constant.32.clone.refs_3_, bf16[64,192]{1,0:T(8,128)(2,1)} %constant.30.clone.refs_4_, ...), custom_call_target="tpu_custom_call" | custom-call | flops 10000000000 | bytes 6000000 | tf_op jit(solution)/shard_map/pallas_call | solution.py:157
  37.5 0.0 copy-done.7
  37.5 0.0 all-to-all-done.1
  37.5 0.0 copy-start.1
  37.5 7.0 %all-to-all-start = ((bf16[16,8,2176]{2,1,0:T(8,128)(2,1)}), bf16[16,8,2176]{2,1,0:T(8,128)(2,1)S(1)}, u32[]{:S(2)}, u32[]{:S(2)}) async-start(bf16[16,8,2176]{2,1,0:T(8,128)(2,1)} %shard_map.166), calls=%async_computation | async-start | bytes 1114112 | tf_op jit(solution)/shard_map/all_to_all | solution.py:446
  44.5 0.0 collective-permute-done.1.refs_2_
  44.5 0.0 copy-start.8
  44.5 0.4 collective-permute-start.5
  44.9 1.2 collective-permute-start.14
  46.1 0.0 collective-permute-done.3.refs_4_
  46.1 1.6 %collective-permute-start.15 = (bf16[128,2176]{1,0:T(8,128)(2,1)S(1)}, bf16[128,2176]{1,0:T(8,128)(2,1)}, u32[]{:S(2)}, u32[]{:S(2)}) collective-permute-start(bf16[128,2176]{1,0:T(8,128)(2,1)S(1)} %bitcast.18), channel_id=1, source_target_pairs={{0,6},{1,7},{2,0},{3,1},{4,2},{5,3},{6,4},{7,5},{8,14},{9,15},{10,... | collective-permute-start | bytes 1671176 | tf_op jit(solution)/shard_map/ppermute | solution.py:415
  47.6 0.0 collective-permute-done.2.refs_3_
  47.6 0.7 collective-permute-start.17
  48.3 6.5 %all-to-all-done = bf16[16,8,2176]{2,1,0:T(8,128)(2,1)S(1)} async-done(((bf16[16,8,2176]{2,1,0:T(8,128)(2,1)}), bf16[16,8,2176]{2,1,0:T(8,128)(2,1)S(1)}, u32[]{:S(2)}, u32[]{:S(2)}) %all-to-all-start) | async-done | bytes 557088 | tf_op jit(solution)/shard_map/all_to_all | solution.py:446
  54.9 0.0 collective-permute-done.4.refs_5_
  54.9 2.7 %collective-permute-start.8 = (bf16[128,2176]{1,0:T(8,128)(2,1)S(1)}, bf16[128,2176]{1,0:T(8,128)(2,1)S(1)}, u32[]{:S(2)}, u32[]{:S(2)}) collective-permute-start(bf16[128,2176]{1,0:T(8,128)(2,1)S(1)} %bitcast.10), channel_id=1, source_target_pairs={{0,6},{1,7},{2,0},{3,1},{4,2},{5,3},{6,4},{7,5},{8,14},{9,15},{10,... | collective-permute-start | bytes 1671176 | tf_op jit(solution)/shard_map/ppermute | solution.py:415
  57.6 0.0 collective-permute-done.5.refs_6_
  57.6 0.0 collective-permute-start.7
  57.6 2.6 %collective-permute-done.14.refs_3_ = bf16[128,2176]{1,0:T(8,128)(2,1)} collective-permute-done((bf16[128,2176]{1,0:T(8,128)(2,1)S(1)}, bf16[128,2176]{1,0:T(8,128)(2,1)}, u32[]{:S(2)}, u32[]{:S(2)}) %collective-permute-start.14) | collective-permute-done | bytes 557088 | tf_op jit(solution)/shard_map/ppermute | solution.py:415
  60.2 0.0 collective-permute-start.16
  60.2 0.0 collective-permute-done.15.refs_4_
  60.2 2.0 %collective-permute-start.18 = (bf16[128,2176]{1,0:T(8,128)(2,1)}, bf16[128,2176]{1,0:T(8,128)(2,1)}, u32[]{:S(2)}, u32[]{:S(2)}) collective-permute-start(bf16[128,2176]{1,0:T(8,128)(2,1)} %collective-permute-done.14.refs_3_), channel_id=1, source_target_pairs={{0,1},{1,0},{2,3},{3,2},{4,5},{5,4},{6,7},{7,6},{8,9},{9,8},{10,11... | collective-permute-start | bytes 1671176 | tf_op jit(solution)/shard_map/ppermute | solution.py:419
  62.2 0.0 collective-permute-done.17.refs_6_
  62.2 0.1 collective-permute-start.19
  62.3 9.4 %collective-permute-done.8.refs_4_.refs_12_ = bf16[128,2176]{1,0:T(8,128)(2,1)S(1)} collective-permute-done((bf16[128,2176]{1,0:T(8,128)(2,1)S(1)}, bf16[128,2176]{1,0:T(8,128)(2,1)S(1)}, u32[]{:S(2)}, u32[]{:S(2)}) %collective-permute-start.8) | collective-permute-done | bytes 557088 | tf_op jit(solution)/shard_map/ppermute | solution.py:415
  71.7 2.9 %collective-permute-start.9 = (bf16[128,2176]{1,0:T(8,128)(2,1)S(1)}, bf16[128,2176]{1,0:T(8,128)(2,1)S(1)}, u32[]{:S(2)}, u32[]{:S(2)}) collective-permute-start(bf16[128,2176]{1,0:T(8,128)(2,1)S(1)} %collective-permute-done.8.refs_4_.refs_12_), channel_id=1, source_target_pairs={{0,6},{1,7},{2,0},{3,1},{4,2},{5,3},{6,4},{7,5},{8,14},{9,15},{10,... | collective-permute-start | bytes 1671176 | tf_op jit(solution)/shard_map/ppermute | solution.py:415
  74.5 0.0 collective-permute-done.7.refs_3_.refs_11_
  74.5 2.4 %collective-permute-start.6 = (bf16[64,4096]{1,0:T(8,128)(2,1)}, bf16[64,4096]{1,0:T(8,128)(2,1)}, u32[]{:S(2)}, u32[]{:S(2)}) collective-permute-start(bf16[64,4096]{1,0:T(8,128)(2,1)} %collective-permute-done.2.refs_3_), channel_id=1, source_target_pairs={{0,1},{1,0},{2,3},{3,2},{4,5},{5,4},{6,7},{7,6},{8,9},{9,8},{10,11... | collective-permute-start | bytes 1572872 | tf_op jit(solution)/shard_map/ppermute | solution.py:419
  77.0 1.9 %collective-permute-done.6.refs_7_ = bf16[64,4096]{1,0:T(8,128)(2,1)} collective-permute-done((bf16[64,4096]{1,0:T(8,128)(2,1)}, bf16[64,4096]{1,0:T(8,128)(2,1)}, u32[]{:S(2)}, u32[]{:S(2)}) %collective-permute-start.6) | collective-permute-done | bytes 524320 | tf_op jit(solution)/shard_map/ppermute | solution.py:419
  78.8 0.4 collective-permute-start.10
  79.2 3.1 %collective-permute-done.16.refs_5_ = bf16[128,2176]{1,0:T(8,128)(2,1)} collective-permute-done((bf16[128,2176]{1,0:T(8,128)(2,1)}, bf16[128,2176]{1,0:T(8,128)(2,1)}, u32[]{:S(2)}, u32[]{:S(2)}) %collective-permute-start.16) | collective-permute-done | bytes 557088 | tf_op jit(solution)/shard_map/ppermute | solution.py:415
  82.3 3.5 %collective-permute-start.12 = (bf16[128,2176]{1,0:T(8,128)(2,1)S(1)}, bf16[128,2176]{1,0:T(8,128)(2,1)}, u32[]{:S(2)}, u32[]{:S(2)}) collective-permute-start(bf16[128,2176]{1,0:T(8,128)(2,1)S(1)} %collective-permute-done.8.refs_4_.refs_12_), channel_id=1, source_target_pairs={{0,1},{1,0},{2,3},{3,2},{4,5},{5,4},{6,7},{7,6},{8,9},{9,8},{10,11... | collective-permute-start | bytes 1671176 | tf_op jit(solution)/shard_map/ppermute | solution.py:419
  85.9 0.0 collective-permute-done.18.refs_7_
  85.9 0.0 collective-permute-start.11
  85.9 0.0 collective-permute-done.19.refs_8_
  85.9 0.5 collective-permute-start.20
  86.4 0.0 collective-permute-done.9.refs_5_.refs_13_
  86.4 1.0 collective-permute-start.13
  87.4 5.4 %score0.1.begun_ref = f32[512,128]{1,0:T(8,128)} custom-call(bf16[128,2176]{1,0:T(8,128)(2,1)} %bitcast.20, bf16[128,2176]{1,0:T(8,128)(2,1)} %bitcast.21, bf16[64,4096]{1,0:T(8,128)(2,1)} %copy-done.2, bf16[64,4096]{1,0:T(8,128)(2,1)} %copy-done.7, bf16[64,4096]{1,0:T(8,128)(2,1)} %copy-done.8, bf16[64,4096]{1,0:T(8,128)(2,1)} %collective-permute-done.2.refs_3_, ...), custom_call_target="tpu_custom_call" | custom-call | flops 1000000000 | bytes 5000000 | tf_op jit(solution)/shard_map/score0/pallas_call | solution.py:226
  92.8 0.0 copy-done
  92.8 3.4 %score1.1 = (f32[16,40,128]{2,1,0:T(8,128)}, f32[16,128]{1,0:T(8,128)}) custom-call(s32[1]{0:T(128)} %bitcast.1.col_ref.refs_0_, bf16[128,2176]{1,0:T(8,128)(2,1)} %bitcast.13, bf16[128,2176]{1,0:T(8,128)(2,1)} %bitcast.14, f32[1,8]{1,0:T(1,128)} %bitcast.25, f32[512,128]{1,0:T(8,128)} %score0.1.begun_ref, bf16[64,4096]{1,0:T(8,128)(2,1)} %copy-done.2, ...), custom_call_target="tpu_custom_call" | custom-call | flops 1000000000 | bytes 4000000 | tf_op jit(solution)/shard_map/score1/pallas_call | solution.py:283
  96.2 15.3 %all_to_all.20.parts_ref = f32[16,40,128]{2,1,0:T(8,128)} all-to-all(f32[16,40,128]{2,1,0:T(8,128)} %get-tuple-element.9), channel_id=1, replica_groups=mesh['tomo'=16,'cls'=8] {'tomo'}, dimensions={0} | all-to-all | bytes 655360 | tf_op jit(solution)/shard_map/all_to_all | solution.py:454
  111.5 1.9 %weights.1 = (f32[8,32]{1,0:T(8,128)}, bf16[8,64,128]{2,1,0:T(8,128)(2,1)}) custom-call(s32[1]{0:T(128)} %bitcast.at_ref, f32[16,40,128]{2,1,0:T(8,128)} %all_to_all.20.parts_ref, f32[16,128]{1,0:T(8,128)} %get-tuple-element.10.codes_ref), custom_call_target="tpu_custom_call" | custom-call | tf_op jit(solution)/shard_map/weights/pallas_call | solution.py:345
  113.4 12.3 %all_to_all.21.refs_1_ = bf16[8,64,128]{2,1,0:T(8,128)(2,1)} all-to-all(bf16[8,64,128]{2,1,0:T(8,128)(2,1)} %get-tuple-element.12), channel_id=1, replica_groups=mesh['tomo'=16,'cls'=8] {'cls'}, dimensions={0} | all-to-all | bytes 262144 | tf_op jit(solution)/shard_map/all_to_all | solution.py:456
  125.7 0.0 collective-permute-done.20.refs_9_
  125.7 3.4 %shard_map.168.refs_18_ = f32[64,4096]{1,0:T(8,128)} custom-call(s32[1]{0:T(128)} %bitcast.1.col_ref.refs_0_, bf16[8,64,128]{2,1,0:T(8,128)(2,1)} %all_to_all.21.refs_1_, bf16[128,2176]{1,0:T(8,128)(2,1)} %bitcast.22, bf16[128,2176]{1,0:T(8,128)(2,1)} %collective-permute-done.14.refs_3_, bf16[128,2176]{1,0:T(8,128)(2,1)} %collective-permute-done.15.refs_4_, ...), custom_call_target="tpu_custom_call" | custom-call | flops 300000000 | bytes 5000000 | tf_op jit(solution)/shard_map/pallas_call | solution.py:399
  129.1 0.0 collective-permute-done.10.refs_6_.refs_14_
  129.1 0.0 collective-permute-done.12.refs_8_.refs_16_
  129.2 0.0 collective-permute-done.11.refs_7_.refs_15_
  129.2 0.0 collective-permute-done.13.refs_9_.refs_17_
  129.2 0.8 copy-done.6
  130.0 3.5 %shard_map.169 = (f32[64,4096]{1,0:T(8,128)}, f32[64,64]{1,0:T(8,128)}) custom-call(s32[1]{0:T(128)} %bitcast.1.col_ref.refs_0_, bf16[8,64,128]{2,1,0:T(8,128)(2,1)} %all_to_all.21.refs_1_, bf16[128,2176]{1,0:T(8,128)(2,1)} %bitcast.15, bf16[128,2176]{1,0:T(8,128)(2,1)} %copy-done.4, bf16[128,2176]{1,0:T(8,128)(2,1)} %copy-done.3, ...), custom_call_target="tpu_custom_call", output_to_operand_aliasing={{0}: (18, {})} | custom-call | flops 300000000 | bytes 5000000 | tf_op jit(solution)/shard_map/pallas_call | solution.py:399
  (12 shorter events, 0.0 us)
Async XLA Ops:
  1.7 16.0 %copy-start.2 = (bf16[64,4096]{1,0:T(8,128)(2,1)}, bf16[64,4096]{1,0:T(8,128)(2,1)S(1)}, u32[]{:S(2)}) copy-start(bf16[64,4096]{1,0:T(8,128)(2,1)S(1)} %constant_dynamic-slice_fusion.refs_0_) | copy-start | bytes 1572868
  1.7 23.9 %collective-permute-start = (bf16[64,4096]{1,0:T(8,128)(2,1)S(1)}, bf16[64,4096]{1,0:T(8,128)(2,1)S(1)}, u32[]{:S(2)}, u32[]{:S(2)}) collective-permute-start(bf16[64,4096]{1,0:T(8,128)(2,1)S(1)} %constant_dynamic-slice_fusion.refs_0_), channel_id=1, source_target_pairs={{0,2},{1,3},{2,4},{3,5},{4,6},{5,7},{6,0},{7,1},{8,10},{9,11},{10,... | collective-permute-start | bytes 1572872 | tf_op jit(solution)/shard_map/ppermute | solution.py:415
  3.8 40.7 %collective-permute-start.1 = (bf16[64,4096]{1,0:T(8,128)(2,1)S(1)}, bf16[64,4096]{1,0:T(8,128)(2,1)S(1)}, u32[]{:S(2)}, u32[]{:S(2)}) collective-permute-start(bf16[64,4096]{1,0:T(8,128)(2,1)S(1)} %constant_dynamic-slice_fusion.refs_0_), channel_id=1, source_target_pairs={{0,6},{1,7},{2,0},{3,1},{4,2},{5,3},{6,4},{7,5},{8,14},{9,15},{10,... | collective-permute-start | bytes 1572872 | tf_op jit(solution)/shard_map/ppermute | solution.py:415
  5.2 40.9 %collective-permute-start.3 = (bf16[64,4096]{1,0:T(8,128)(2,1)S(1)}, bf16[64,4096]{1,0:T(8,128)(2,1)S(1)}, u32[]{:S(2)}, u32[]{:S(2)}) collective-permute-start(bf16[64,4096]{1,0:T(8,128)(2,1)S(1)} %constant_dynamic-slice_fusion.refs_0_), channel_id=1, source_target_pairs={{0,1},{1,0},{2,3},{3,2},{4,5},{5,4},{6,7},{7,6},{8,9},{9,8},{10,11... | collective-permute-start | bytes 1572872 | tf_op jit(solution)/shard_map/ppermute | solution.py:419
  17.7 19.8 %all-to-all-start.1 = ((bf16[16,8,2176]{2,1,0:T(8,128)(2,1)}), bf16[16,8,2176]{2,1,0:T(8,128)(2,1)S(1)}, u32[]{:S(2)}, u32[]{:S(2)}) async-start(bf16[16,8,2176]{2,1,0:T(8,128)(2,1)} %shard_map.167), calls=%async_computation.1 | async-start | bytes 1114112 | tf_op jit(solution)/shard_map/all_to_all | solution.py:446
  25.6 11.9 %copy-start.7 = (bf16[64,4096]{1,0:T(8,128)(2,1)}, bf16[64,4096]{1,0:T(8,128)(2,1)S(1)}, u32[]{:S(2)}) copy-start(bf16[64,4096]{1,0:T(8,128)(2,1)S(1)} %collective-permute-done.refs_1_) | copy-start | bytes 1572868
  25.6 22.0 %collective-permute-start.2 = (bf16[64,4096]{1,0:T(8,128)(2,1)S(1)}, bf16[64,4096]{1,0:T(8,128)(2,1)}, u32[]{:S(2)}, u32[]{:S(2)}) collective-permute-start(bf16[64,4096]{1,0:T(8,128)(2,1)S(1)} %collective-permute-done.refs_1_), channel_id=1, source_target_pairs={{0,2},{1,3},{2,4},{3,5},{4,6},{5,7},{6,0},{7,1},{8,10},{9,11},{10,... | collective-permute-start | bytes 1572872 | tf_op jit(solution)/shard_map/ppermute | solution.py:415
  25.7 29.2 %collective-permute-start.4 = (bf16[64,4096]{1,0:T(8,128)(2,1)S(1)}, bf16[64,4096]{1,0:T(8,128)(2,1)}, u32[]{:S(2)}, u32[]{:S(2)}) collective-permute-start(bf16[64,4096]{1,0:T(8,128)(2,1)S(1)} %collective-permute-done.refs_1_), channel_id=1, source_target_pairs={{0,1},{1,0},{2,3},{3,2},{4,5},{5,4},{6,7},{7,6},{8,9},{9,8},{10,11... | collective-permute-start | bytes 1572872 | tf_op jit(solution)/shard_map/ppermute | solution.py:419
  37.5 49.9 %copy-start.1 = (bf16[16,8,2176]{2,1,0:T(8,128)(2,1)}, bf16[16,8,2176]{2,1,0:T(8,128)(2,1)S(1)}, u32[]{:S(2)}) copy-start(bf16[16,8,2176]{2,1,0:T(8,128)(2,1)S(1)} %all-to-all-done.1) | copy-start | bytes 1671172
  37.5 17.4 %all-to-all-start = ((bf16[16,8,2176]{2,1,0:T(8,128)(2,1)}), bf16[16,8,2176]{2,1,0:T(8,128)(2,1)S(1)}, u32[]{:S(2)}, u32[]{:S(2)}) async-start(bf16[16,8,2176]{2,1,0:T(8,128)(2,1)} %shard_map.166), calls=%async_computation | async-start | bytes 1114112 | tf_op jit(solution)/shard_map/all_to_all | solution.py:446
  44.5 13.1 %copy-start.8 = (bf16[64,4096]{1,0:T(8,128)(2,1)}, bf16[64,4096]{1,0:T(8,128)(2,1)S(1)}, u32[]{:S(2)}) copy-start(bf16[64,4096]{1,0:T(8,128)(2,1)S(1)} %collective-permute-done.1.refs_2_) | copy-start | bytes 1572868
  44.5 13.1 %collective-permute-start.5 = (bf16[64,4096]{1,0:T(8,128)(2,1)S(1)}, bf16[64,4096]{1,0:T(8,128)(2,1)}, u32[]{:S(2)}, u32[]{:S(2)}) collective-permute-start(bf16[64,4096]{1,0:T(8,128)(2,1)S(1)} %collective-permute-done.1.refs_2_), channel_id=1, source_target_pairs={{0,1},{1,0},{2,3},{3,2},{4,5},{5,4},{6,7},{7,6},{8,9},{9,8},{10,11... | collective-permute-start | bytes 1572872 | tf_op jit(solution)/shard_map/ppermute | solution.py:419
  44.9 15.3 %collective-permute-start.14 = (bf16[128,2176]{1,0:T(8,128)(2,1)S(1)}, bf16[128,2176]{1,0:T(8,128)(2,1)}, u32[]{:S(2)}, u32[]{:S(2)}) collective-permute-start(bf16[128,2176]{1,0:T(8,128)(2,1)S(1)} %bitcast.17), channel_id=1, source_target_pairs={{0,2},{1,3},{2,4},{3,5},{4,6},{5,7},{6,0},{7,1},{8,10},{9,11},{10,... | collective-permute-start | bytes 1671176 | tf_op jit(solution)/shard_map/ppermute | solution.py:415
  46.1 16.2 %copy-start.9 = (bf16[64,4096]{1,0:T(8,128)(2,1)}, bf16[64,4096]{1,0:T(8,128)(2,1)S(1)}, u32[]{:S(2)}) copy-start(bf16[64,4096]{1,0:T(8,128)(2,1)S(1)} %collective-permute-done.3.refs_4_) | copy-start | bytes 1572868
  46.1 14.1 %collective-permute-start.15 = (bf16[128,2176]{1,0:T(8,128)(2,1)S(1)}, bf16[128,2176]{1,0:T(8,128)(2,1)}, u32[]{:S(2)}, u32[]{:S(2)}) collective-permute-start(bf16[128,2176]{1,0:T(8,128)(2,1)S(1)} %bitcast.18), channel_id=1, source_target_pairs={{0,6},{1,7},{2,0},{3,1},{4,2},{5,3},{6,4},{7,5},{8,14},{9,15},{10,... | collective-permute-start | bytes 1671176 | tf_op jit(solution)/shard_map/ppermute | solution.py:415
  47.6 14.5 %collective-permute-start.17 = (bf16[128,2176]{1,0:T(8,128)(2,1)S(1)}, bf16[128,2176]{1,0:T(8,128)(2,1)}, u32[]{:S(2)}, u32[]{:S(2)}) collective-permute-start(bf16[128,2176]{1,0:T(8,128)(2,1)S(1)} %bitcast.19), channel_id=1, source_target_pairs={{0,1},{1,0},{2,3},{3,2},{4,5},{5,4},{6,7},{7,6},{8,9},{9,8},{10,11... | collective-permute-start | bytes 1671176 | tf_op jit(solution)/shard_map/ppermute | solution.py:419
  54.9 37.9 %copy-start = (bf16[16,8,2176]{2,1,0:T(8,128)(2,1)}, bf16[16,8,2176]{2,1,0:T(8,128)(2,1)S(1)}, u32[]{:S(2)}) copy-start(bf16[16,8,2176]{2,1,0:T(8,128)(2,1)S(1)} %all-to-all-done) | copy-start | bytes 1671172
  54.9 16.8 %collective-permute-start.8 = (bf16[128,2176]{1,0:T(8,128)(2,1)S(1)}, bf16[128,2176]{1,0:T(8,128)(2,1)S(1)}, u32[]{:S(2)}, u32[]{:S(2)}) collective-permute-start(bf16[128,2176]{1,0:T(8,128)(2,1)S(1)} %bitcast.10), channel_id=1, source_target_pairs={{0,6},{1,7},{2,0},{3,1},{4,2},{5,3},{6,4},{7,5},{8,14},{9,15},{10,... | collective-permute-start | bytes 1671176 | tf_op jit(solution)/shard_map/ppermute | solution.py:415
  57.6 17.0 %collective-permute-start.7 = (bf16[128,2176]{1,0:T(8,128)(2,1)S(1)}, bf16[128,2176]{1,0:T(8,128)(2,1)S(1)}, u32[]{:S(2)}, u32[]{:S(2)}) collective-permute-start(bf16[128,2176]{1,0:T(8,128)(2,1)S(1)} %bitcast.11), channel_id=1, source_target_pairs={{0,2},{1,3},{2,4},{3,5},{4,6},{5,7},{6,0},{7,1},{8,10},{9,11},{10,... | collective-permute-start | bytes 1671176 | tf_op jit(solution)/shard_map/ppermute | solution.py:415
  60.2 22.2 %collective-permute-start.16 = (bf16[128,2176]{1,0:T(8,128)(2,1)}, bf16[128,2176]{1,0:T(8,128)(2,1)}, u32[]{:S(2)}, u32[]{:S(2)}) collective-permute-start(bf16[128,2176]{1,0:T(8,128)(2,1)} %collective-permute-done.14.refs_3_), channel_id=1, source_target_pairs={{0,2},{1,3},{2,4},{3,5},{4,6},{5,7},{6,0},{7,1},{8,10},{9,11},{10,... | collective-permute-start | bytes 1671176 | tf_op jit(solution)/shard_map/ppermute | solution.py:415
  60.2 25.7 %collective-permute-start.18 = (bf16[128,2176]{1,0:T(8,128)(2,1)}, bf16[128,2176]{1,0:T(8,128)(2,1)}, u32[]{:S(2)}, u32[]{:S(2)}) collective-permute-start(bf16[128,2176]{1,0:T(8,128)(2,1)} %collective-permute-done.14.refs_3_), channel_id=1, source_target_pairs={{0,1},{1,0},{2,3},{3,2},{4,5},{5,4},{6,7},{7,6},{8,9},{9,8},{10,11... | collective-permute-start | bytes 1671176 | tf_op jit(solution)/shard_map/ppermute | solution.py:419
  62.2 23.7 %collective-permute-start.19 = (bf16[128,2176]{1,0:T(8,128)(2,1)}, bf16[128,2176]{1,0:T(8,128)(2,1)}, u32[]{:S(2)}, u32[]{:S(2)}) collective-permute-start(bf16[128,2176]{1,0:T(8,128)(2,1)} %collective-permute-done.15.refs_4_), channel_id=1, source_target_pairs={{0,1},{1,0},{2,3},{3,2},{4,5},{5,4},{6,7},{7,6},{8,9},{9,8},{10,11... | collective-permute-start | bytes 1671176 | tf_op jit(solution)/shard_map/ppermute | solution.py:419
  71.7 57.4 %copy-start.3 = (bf16[128,2176]{1,0:T(8,128)(2,1)}, bf16[128,2176]{1,0:T(8,128)(2,1)S(1)}, u32[]{:S(2)}) copy-start(bf16[128,2176]{1,0:T(8,128)(2,1)S(1)} %collective-permute-done.8.refs_4_.refs_12_) | copy-start | bytes 1671172
  71.7 14.7 %collective-permute-start.9 = (bf16[128,2176]{1,0:T(8,128)(2,1)S(1)}, bf16[128,2176]{1,0:T(8,128)(2,1)S(1)}, u32[]{:S(2)}, u32[]{:S(2)}) collective-permute-start(bf16[128,2176]{1,0:T(8,128)(2,1)S(1)} %collective-permute-done.8.refs_4_.refs_12_), channel_id=1, source_target_pairs={{0,6},{1,7},{2,0},{3,1},{4,2},{5,3},{6,4},{7,5},{8,14},{9,15},{10,... | collective-permute-start | bytes 1671176 | tf_op jit(solution)/shard_map/ppermute | solution.py:415
  74.5 54.6 %copy-start.4 = (bf16[128,2176]{1,0:T(8,128)(2,1)}, bf16[128,2176]{1,0:T(8,128)(2,1)S(1)}, u32[]{:S(2)}) copy-start(bf16[128,2176]{1,0:T(8,128)(2,1)S(1)} %collective-permute-done.7.refs_3_.refs_11_) | copy-start | bytes 1671172
  74.5 4.3 %collective-permute-start.6 = (bf16[64,4096]{1,0:T(8,128)(2,1)}, bf16[64,4096]{1,0:T(8,128)(2,1)}, u32[]{:S(2)}, u32[]{:S(2)}) collective-permute-start(bf16[64,4096]{1,0:T(8,128)(2,1)} %collective-permute-done.2.refs_3_), channel_id=1, source_target_pairs={{0,1},{1,0},{2,3},{3,2},{4,5},{5,4},{6,7},{7,6},{8,9},{9,8},{10,11... | collective-permute-start | bytes 1572872 | tf_op jit(solution)/shard_map/ppermute | solution.py:419
  78.8 50.3 %collective-permute-start.10 = (bf16[128,2176]{1,0:T(8,128)(2,1)S(1)}, bf16[128,2176]{1,0:T(8,128)(2,1)S(1)}, u32[]{:S(2)}, u32[]{:S(2)}) collective-permute-start(bf16[128,2176]{1,0:T(8,128)(2,1)S(1)} %bitcast.12), channel_id=1, source_target_pairs={{0,1},{1,0},{2,3},{3,2},{4,5},{5,4},{6,7},{7,6},{8,9},{9,8},{10,11... | collective-permute-start | bytes 1671176 | tf_op jit(solution)/shard_map/ppermute | solution.py:419
  82.3 46.8 %collective-permute-start.12 = (bf16[128,2176]{1,0:T(8,128)(2,1)S(1)}, bf16[128,2176]{1,0:T(8,128)(2,1)}, u32[]{:S(2)}, u32[]{:S(2)}) collective-permute-start(bf16[128,2176]{1,0:T(8,128)(2,1)S(1)} %collective-permute-done.8.refs_4_.refs_12_), channel_id=1, source_target_pairs={{0,1},{1,0},{2,3},{3,2},{4,5},{5,4},{6,7},{7,6},{8,9},{9,8},{10,11... | collective-permute-start | bytes 1671176 | tf_op jit(solution)/shard_map/ppermute | solution.py:419
  85.9 43.3 %collective-permute-start.11 = (bf16[128,2176]{1,0:T(8,128)(2,1)S(1)}, bf16[128,2176]{1,0:T(8,128)(2,1)}, u32[]{:S(2)}, u32[]{:S(2)}) collective-permute-start(bf16[128,2176]{1,0:T(8,128)(2,1)S(1)} %collective-permute-done.7.refs_3_.refs_11_), channel_id=1, source_target_pairs={{0,1},{1,0},{2,3},{3,2},{4,5},{5,4},{6,7},{7,6},{8,9},{9,8},{10,11... | collective-permute-start | bytes 1671176 | tf_op jit(solution)/shard_map/ppermute | solution.py:419
  85.9 39.8 %collective-permute-start.20 = (bf16[128,2176]{1,0:T(8,128)(2,1)}, bf16[128,2176]{1,0:T(8,128)(2,1)}, u32[]{:S(2)}, u32[]{:S(2)}) collective-permute-start(bf16[128,2176]{1,0:T(8,128)(2,1)} %collective-permute-done.16.refs_5_), channel_id=1, source_target_pairs={{0,1},{1,0},{2,3},{3,2},{4,5},{5,4},{6,7},{7,6},{8,9},{9,8},{10,11... | collective-permute-start | bytes 1671176 | tf_op jit(solution)/shard_map/ppermute | solution.py:419
  86.4 42.7 %copy-start.5 = (bf16[128,2176]{1,0:T(8,128)(2,1)}, bf16[128,2176]{1,0:T(8,128)(2,1)S(1)}, u32[]{:S(2)}) copy-start(bf16[128,2176]{1,0:T(8,128)(2,1)S(1)} %collective-permute-done.9.refs_5_.refs_13_) | copy-start | bytes 1671172
  86.4 42.8 %collective-permute-start.13 = (bf16[128,2176]{1,0:T(8,128)(2,1)S(1)}, bf16[128,2176]{1,0:T(8,128)(2,1)}, u32[]{:S(2)}, u32[]{:S(2)}) collective-permute-start(bf16[128,2176]{1,0:T(8,128)(2,1)S(1)} %collective-permute-done.9.refs_5_.refs_13_), channel_id=1, source_target_pairs={{0,1},{1,0},{2,3},{3,2},{4,5},{5,4},{6,7},{7,6},{8,9},{9,8},{10,11... | collective-permute-start | bytes 1671176 | tf_op jit(solution)/shard_map/ppermute | solution.py:419
  129.1 0.8 copy-start.6
